TPU v7x, 256 devices: a whole 4x4x8 slice. The times are simulated.
256 devices in a mesh: dev: 128 (over z, y, x_hi, core), rhs: 2 (over x_lo).
Axes of the slice: x: 4 (x_hi: 2, x_lo: 2; x = x_hi * 2 + x_lo), y: 4, z: 8, core: 2. Of those that a mesh axis runs over, the one named last changes fastest.
Arguments:
- top_adj: float32 [16, 256, 128, 256], P('rhs', 'dev'), may hold values from -6 to 6
- level1_adj: float32 [16, 128, 512, 128], P('rhs', 'dev'), may hold values from -6 to 6
- image_offsets: int32 [64, 2], P('rhs'), may hold values from -6 to 6
- image_weights: float32 [64], P('rhs'), may hold values from 0.2 to 1
- incidence: float32 [16, 2], replicated, may hold values from -0.6 to 0.6
- child_list: int32 [128, 4], replicated, may hold values from 0 to 511, as said below
- theta_index_top: int32 [128, 3], replicated, may hold values from 0 to 63
- theta_weight_top: float32 [128, 3], replicated, may hold values from -2.7 to 2.7
- phi_weight_top: float32 [256, 3], replicated, may hold values from -2.7 to 2.7
- theta_index_mid: int32 [64, 3], replicated, may hold values from 0 to 31
- theta_weight_mid: float32 [64, 3], replicated, may hold values from -2.7 to 2.7
- phi_weight_mid: float32 [128, 3], replicated, may hold values from -2.7 to 2.7
Outputs:
- level0_adj: float32 [16, 2048, 4096], P('rhs', 'dev')
Inputs may be any that keep to these rules, and one draw needn't show every extreme that they name: `child_list`: row b holds the middle-level boxes 4 b to 4 b + 3, each once.
All inputs are finite; a program needn't handle non-finite values.
Results may differ from a plain program's by a relative error of at most 0.0003.
Values sent between devices are 32-bit elements; how exact they have to be, the bound alone decides.
A program may use at most 128 MiB of HBM per device.

v0:
```python
import math

import jax
import jax.numpy as jnp
from jax import lax
from jax.sharding import PartitionSpec as P

PHASE_TOP = 18.85
PHASE_MID = 9.42
LATTICE = 12.57


def side_by_side(arrays, axis, dim, along):
    widths = [math.prod(a.shape[along:]) for a in arrays]
    both = jnp.concatenate(
        [a.reshape(*a.shape[:along], w) for a, w in zip(arrays, widths)], axis=along
    )
    out = lax.all_gather(both, axis, axis=dim, tiled=True)
    tiles = jnp.split(out, [sum(widths[:k]) for k in range(1, len(widths))], axis=along)
    return tuple((b.reshape(*out.shape[:along], *a.shape[along:]) for a, b in zip(arrays, tiles)))


def directions(theta_count, phi_ids, phi_count):
    theta = math.pi / theta_count * (jnp.arange(theta_count, dtype=jnp.float32) + 0.5)
    azimuth = 2.0 * math.pi / phi_count * phi_ids.astype(jnp.float32)
    sin_theta = jnp.sin(theta)
    along_x = jnp.cos(azimuth)[:, None] * sin_theta[None, :]
    along_y = jnp.sin(azimuth)[:, None] * sin_theta[None, :]
    along_z = jnp.cos(theta)
    return (along_x, along_y, along_z)


def theta_matrix(index, weight, columns):
    hits = (index[:, :, None] == jnp.arange(columns, dtype=jnp.int32)[None, None, :]).astype(
        jnp.float32
    )
    return jnp.sum(weight[:, :, None] * hits, axis=1)


def phi_matrix(weight, row_ids, coarse_count, column_ids):
    target = (row_ids[:, None] // 2 + jnp.arange(3, dtype=jnp.int32)[None, :] - 1) % coarse_count
    hits = (target[:, :, None] == column_ids[None, None, :]).astype(jnp.float32)
    return jnp.sum(weight[:, :, None] * hits, axis=1)


def octant_phase(factor, octant, along_x, along_y, along_z):
    sign_x = 2.0 * (octant % 2) - 1.0
    sign_y = 2.0 * (octant // 2) - 1.0
    angle = factor * (sign_x * along_x + sign_y * along_y - along_z[None, :])
    return (jnp.cos(angle), jnp.sin(angle))


def lattice_sum(offsets, weighted, incident, along_x, along_y):
    phase_arg = LATTICE * (
        offsets[:, 0, None, None, None] * (along_x[None, None] - incident[None, :, 0, None, None])
        + offsets[:, 1, None, None, None] * (along_y[None, None] - incident[None, :, 1, None, None])
    )
    sum_real = jnp.sum(weighted[:, None, None, None] * jnp.cos(phase_arg), axis=0)
    sum_imag = jnp.sum(weighted[:, None, None, None] * jnp.sin(phase_arg), axis=0)
    return (sum_real, sum_imag)


def upper_level(
    top_real, top_imag, along_x, along_y, along_z, theta_map, phi_map, children, top_ids
):
    summed = None
    for octant in range(4):
        cosine, sine = octant_phase(PHASE_TOP, octant, along_x, along_y, along_z)
        cosine = cosine[:, None, :]
        sine = sine[:, None, :]
        stacked = jnp.stack(
            [top_real * cosine - top_imag * sine, top_real * sine + top_imag * cosine]
        )
        theta_done = jnp.einsum(
            "...pbt,tu->...pbu", stacked, theta_map, precision=lax.Precision.HIGHEST
        )
        phi_done = jnp.einsum(
            "...pbu,pq->...qbu", theta_done, phi_map, precision=lax.Precision.HIGHEST
        )
        select_map = (
            children[:, octant][:, None] - 4 * top_ids[:, None]
            == jnp.arange(4, dtype=jnp.int32)[None, :]
        ).astype(jnp.float32)
        placed = phi_done[..., None, :] * select_map[:, :, None]
        summed = placed if summed is None else summed + placed
    merged = summed.reshape(summed.shape[:-3] + (summed.shape[-3] * 4, summed.shape[-1]))
    return jnp.concatenate([merged[0], merged[1]], axis=-1)


def lower_level(middle, along_x, along_y, along_z, theta_map, phi_map):
    half_width = middle.shape[-1] // 2
    mid_real = middle[..., :half_width]
    mid_imag = middle[..., half_width:]
    real_parts = []
    imag_parts = []
    for octant in range(4):
        cosine, sine = octant_phase(PHASE_MID, octant, along_x, along_y, along_z)
        cosine = cosine[:, None, :]
        sine = sine[:, None, :]
        real_parts.append(mid_real * cosine - mid_imag * sine)
        imag_parts.append(mid_real * sine + mid_imag * cosine)
    stacked = jnp.stack([jnp.stack(real_parts, axis=-2), jnp.stack(imag_parts, axis=-2)])
    theta_done = jnp.einsum(
        "...pijt,tu->...piju", stacked, theta_map, precision=lax.Precision.HIGHEST
    )
    phi_done = jnp.einsum(
        "c...piju,pq->...ijqcu", theta_done, phi_map, precision=lax.Precision.HIGHEST
    )
    result_shape = phi_done.shape
    return phi_done.reshape(
        result_shape[:-5]
        + (result_shape[-5] * 4, result_shape[-3] * result_shape[-2] * result_shape[-1])
    )


def local(
    top_adj,
    level1_adj,
    image_offsets,
    image_weights,
    incidence,
    child_list,
    theta_index_top,
    theta_weight_top,
    phi_weight_top,
    theta_index_mid,
    theta_weight_mid,
    phi_weight_mid,
):
    dev_count = lax.axis_size("dev")
    dev_index = lax.axis_index("dev")
    rhs_count = lax.axis_size("rhs")
    rhs_index = lax.axis_index("rhs")
    exc_local, phi_local, top_boxes, top_width = top_adj.shape
    theta_top_count = top_width // 2
    theta_mid_count = theta_top_count // 2
    theta_low_count = theta_top_count // 4
    phi_top_count = phi_local * dev_count
    phi_mid_count = phi_top_count // 2
    phi_low_count = phi_top_count // 4
    image_total = image_offsets.shape[0] * rhs_count
    own_phi = dev_index * phi_local + jnp.arange(phi_local, dtype=jnp.int32)
    own_x, own_y, top_z = directions(theta_top_count, own_phi, phi_top_count)
    scaled = image_weights * float(image_total) ** (-0.5)
    offsets, weighted = side_by_side((image_offsets.astype(jnp.float32), scaled), "rhs", 0, 1)
    own_incident = lax.dynamic_slice_in_dim(incidence, rhs_index * exc_local, exc_local, 0)
    sum_real, sum_imag = lattice_sum(offsets, weighted, own_incident, own_x, own_y)
    sum_real = sum_real[:, :, None, :]
    sum_imag = sum_imag[:, :, None, :]
    top_real = top_adj[..., :theta_top_count]
    top_imag = top_adj[..., theta_top_count:]
    shifted = jnp.concatenate(
        [sum_real * top_real + sum_imag * top_imag, sum_real * top_imag - sum_imag * top_real],
        axis=-1,
    )
    theta_top = theta_matrix(theta_index_top, theta_weight_top, theta_mid_count)
    mid_all = jnp.arange(phi_mid_count, dtype=jnp.int32)
    mid_x, mid_y, mid_z = directions(theta_mid_count, mid_all, phi_mid_count)
    theta_mid = theta_matrix(theta_index_mid, theta_weight_mid, theta_low_count)
    phi_mid = phi_matrix(
        phi_weight_mid, mid_all, phi_low_count, jnp.arange(phi_low_count, dtype=jnp.int32)
    )
    given = lax.all_to_all(level1_adj, "dev", split_axis=2, concat_axis=1, tiled=True)
    moved = lax.all_to_all(shifted, "dev", split_axis=2, concat_axis=1, tiled=True)
    every_phi = jnp.arange(phi_top_count, dtype=jnp.int32)
    full_dirs = directions(theta_top_count, every_phi, phi_top_count)
    phi_top = phi_matrix(phi_weight_top, every_phi, phi_mid_count, mid_all)
    local_tops = top_boxes // dev_count
    own_children = lax.dynamic_slice_in_dim(child_list, dev_index * local_tops, local_tops, 0)
    own_tops = dev_index * local_tops + jnp.arange(local_tops, dtype=jnp.int32)
    above = upper_level(
        moved[..., :theta_top_count],
        moved[..., theta_top_count:],
        full_dirs[0],
        full_dirs[1],
        top_z,
        theta_top,
        phi_top,
        own_children,
        own_tops,
    )
    return lower_level(given + above, mid_x, mid_y, mid_z, theta_mid, phi_mid)


def solution(mesh):
    placed = (
        P("rhs", "dev", None, None),
        P("rhs", "dev", None, None),
        P("rhs", None),
        P("rhs"),
        P(),
        P(),
        P(),
        P(),
        P(),
        P(),
        P(),
        P(),
    )
    return jax.shard_map(
        local, mesh=mesh, in_specs=placed, out_specs=P("rhs", "dev", None), check_vma=False
    )
```

profile of v0, /device:TPU:1, one launch (start us, length us, event | category | flops | bytes accessed | tf_op | source)
XLA Modules:
  0.0 183.2 jit_solution(6274949842586017790)
XLA Ops:
  0.1 0.8 constant_dynamic-slice_fusion.1
  0.9 0.7 convert_element_type.133
  1.6 0.7 multiply_bitcast_fusion
  2.3 3.7 %all-gather = f32[2,32,3]{1,2,0:T(4,128)S(1)} all-gather(f32[1,32,3]{1,2,0:T(4,128)S(1)} %maximum_bitcast_fusion.10), channel_id=1, replica_groups=mesh['dev'=128,'rhs'=2] {'rhs'}, dimensions={0}, use_global_device_ids=true | all-gather | bytes 1152 | tf_op jit(solution)/shard_map/all_gather | solution.py:18
  6.1 1.7 fusion.78
  7.9 2.4 %multiply_reduce_fusion.1 = (f32[8,2,128]{2,0,1:T(8,128)S(1)}, f32[8,2,128]{2,0,1:T(8,128)S(1)}) fusion(f32[8,2,128]{2,0,1:T(8,128)S(1)} %get-tuple-element.68, f32[64]{0:T(128)S(1)} %get-tuple-element.62, f32[8,2,128]{2,0,1:T(8,128)S(1)} %get-tuple-element.69, f32[64]{0:T(128)S(1)} %get-tuple-element.63, f32[64]{0:T(128)S(1)} %get-tuple-element.61), kind=kLoop, calls=%fused_computation.51 | loop fusion | flops 1044480 | bytes 33536 | tf_op jit(solution)/shard_map/reduce_sum | solution.py:58
  10.3 1.2 multiply_add_fusion.1
  11.5 1.5 pad_maximum_fusion
  13.0 17.0 %all-to-all-start.1 = ((f32[8,2,128,256]{3,0,1,2:T(8,128)}), f32[8,2,128,256]{3,0,1,2:T(8,128)S(1)}, u32[]{:S(2)}, u32[]{:S(2)}) async-start(f32[8,2,128,256]{3,0,1,2:T(8,128)} %pad_maximum_fusion), calls=%async_computation.1 | async-start | bytes 4194304 | tf_op jit(solution)/shard_map/all_to_all | solution.py:164
  33.2 4.1 %copy.103 = f32[8,1,512,128]{3,0,1,2:T(8,128)} copy(f32[8,1,512,128]{3,2,1,0:T(8,128)} %param.13) | data formatting | bytes 4194304 | tf_op args[1]
  37.7 44.0 %all-to-all-done.1 = f32[8,2,128,256]{3,0,1,2:T(8,128)S(1)} async-done(((f32[8,2,128,256]{3,0,1,2:T(8,128)}), f32[8,2,128,256]{3,0,1,2:T(8,128)S(1)}, u32[]{:S(2)}, u32[]{:S(2)}) %all-to-all-start.1) | async-done | bytes 2097184 | tf_op jit(solution)/shard_map/all_to_all | solution.py:164
  81.7 9.1 %all-to-all-start = ((f32[8,1,512,128]{3,0,1,2:T(8,128)}), f32[8,1,512,128]{3,0,1,2:T(8,128)}, u32[]{:S(2)}, u32[]{:S(2)}) async-start(f32[8,1,512,128]{3,0,1,2:T(8,128)} %copy.103), calls=%async_computation | async-start | bytes 4194304 | tf_op jit(solution)/shard_map/all_to_all | solution.py:163
  91.7 1.9 %fusion.20 = (f32[256,128]{1,0:T(8,128)S(1)}, f32[256,128]{1,0:T(8,128)S(1)}, f32[256,128]{1,0:T(8,128)S(1)}, f32[256,128]{1,0:T(8,128)S(1)}, f32[256,128]{1,0:T...) fusion(f32[128]{0:T(128)S(1)} %fusion.68, f32[256]{0:T(256)S(1)} %get-tuple-element.70, ...), kind=kLoop, calls=%fused_computation.64 | loop fusion | flops 524288 | bytes 1051648 | tf_op jit(solution)/shard_map/cos | solution.py:50
  93.8 1.2 subtract_bitcast_fusion.7
  95.0 2.4 %fusion.4 = f32[2,8,256,64]{2,3,1,0:T(8,128)S(1)} fusion(f32[1,8,256,1,128]{4,2,1,0,3:T(8,128)S(1)} %get-tuple-element.8, f32[1,8,256,1,128]{4,2,1,0,3:T(8,128)S(1)} %get-tuple-element.7, f32[128,64]{0,1:T(8,128)S(1)} %select_reduce_fusion.1), kind=kOutput, calls=%fused_computation.9 | convolution fusion | flops 403177472 | bytes 3178496 | tf_op jit(solution)/shard_map/...pbt,tu->...pbu/dot_general | solution.py:74
  97.4 2.4 %fusion.7 = f32[2,8,256,64]{2,3,1,0:T(8,128)S(1)} fusion(f32[1,8,256,1,128]{4,2,1,3,0:T(8,128)S(1)} %get-tuple-element.31, f32[1,8,256,1,128]{4,2,1,3,0:T(8,128)S(1)} %get-tuple-element.32, f32[128,64]{0,1:T(8,128)S(1)} %select_reduce_fusion.1), kind=kOutput, calls=%fused_computation.13 | convolution fusion | flops 403177472 | bytes 3178496 | tf_op jit(solution)/shard_map/...pbt,tu->...pbu/dot_general | solution.py:74
  99.8 2.4 %fusion.10 = f32[2,8,256,64]{2,3,1,0:T(8,128)S(1)} fusion(f32[1,8,256,1,128]{4,2,1,3,0:T(8,128)S(1)} %get-tuple-element.33, f32[1,8,256,1,128]{4,2,1,3,0:T(8,128)S(1)} %get-tuple-element.34, f32[128,64]{0,1:T(8,128)S(1)} %select_reduce_fusion.1), kind=kOutput, calls=%fused_computation.17 | convolution fusion | flops 403177472 | bytes 3178496 | tf_op jit(solution)/shard_map/...pbt,tu->...pbu/dot_general | solution.py:74
  102.3 2.4 %fusion.13 = f32[2,8,256,64]{2,3,1,0:T(8,128)S(1)} fusion(f32[1,8,256,1,128]{4,2,1,3,0:T(8,128)S(1)} %get-tuple-element.35, f32[1,8,256,1,128]{4,2,1,3,0:T(8,128)S(1)} %get-tuple-element.36, f32[128,64]{0,1:T(8,128)S(1)} %select_reduce_fusion.1), kind=kOutput, calls=%fused_computation.21 | convolution fusion | flops 403177472 | bytes 3178496 | tf_op jit(solution)/shard_map/...pbt,tu->...pbu/dot_general | solution.py:74
  104.7 1.2 convolution_bitcast_fusion.4
  105.9 1.0 convolution_bitcast_fusion.3
  106.9 1.0 convolution_bitcast_fusion.2
  107.9 1.0 convolution_bitcast_fusion.1
  108.9 0.7 multiply_add_fusion
  109.7 1.1 slice_bitcast_fusion.1
  110.8 31.2 %all-to-all-done = f32[8,1,512,128]{3,0,1,2:T(8,128)} async-done(((f32[8,1,512,128]{3,0,1,2:T(8,128)}), f32[8,1,512,128]{3,0,1,2:T(8,128)}, u32[]{:S(2)}, u32[]{:S(2)}) %all-to-all-start) | async-done | bytes 2097184 | tf_op jit(solution)/shard_map/all_to_all | solution.py:163
  142.0 2.0 %copy.110 = f32[8,128,4,128]{1,3,2,0:T(8,128)S(1)} copy(f32[8,128,4,128]{3,0,2,1:T(8,128)} %bitcast.2) | data formatting | bytes 4194304 | tf_op jit(solution)/shard_map/all_to_all | solution.py:163
  144.0 1.6 maximum_add_fusion
  146.0 1.1 subtract_bitcast_fusion.3
  147.7 5.0 %fusion = f32[2,8,128,4,4,32]{2,5,4,3,1,0:T(8,128)S(1)} fusion(f32[1,8,128,4,4,64]{2,5,4,3,1,0:T(8,128)S(1)} %maximum_bitcast_fusion.1, f32[64,32]{0,1:T(8,128)S(1)} %select_reduce_fusion.3, f32[8,128,4,1,64]{1,4,2,0,3:T(8,128)S(1)} %get-tuple-element.28, f32[8,128,4,1,64]{1,4,2,0,3:T(8,128)S(1)} %get-tuple-element.26, ...), kind=kOutput, calls=%fused_computation | convolution fusion | flops 810549248 | bytes 12591104 | tf_op jit(solution)/shard_map/...pijt,tu->...piju/dot_general | solution.py:103
  152.7 5.2 %convolution_bitcast_fusion = f32[8,4,4,64,2,32]{3,5,2,1,0,4:T(8,128)} fusion(f32[2,8,128,4,4,32]{2,5,4,3,1,0:T(8,128)S(1)} %fusion, f32[128,64]{0,1:T(8,128)S(1)} %select_reduce_fusion.2), kind=kOutput, calls=%fused_computation.6 | convolution fusion | flops 805306368 | bytes 6324224 | tf_op jit(solution)/shard_map/c...piju,pq->...ijqcu/dot_general | solution.py:106
  157.9 12.3 %copy.115 = f32[8,4,4,64,2,32]{5,4,3,2,1,0:T(2,128)} copy(f32[8,4,4,64,2,32]{3,5,2,1,0,4:T(8,128)} %convolution_bitcast_fusion) | data formatting | bytes 4194304 | tf_op jit(solution)/shard_map/c...piju,pq->...ijqcu/transpose | solution.py:106
  170.2 13.0 %reshape.1488 = f32[8,16,4096]{2,1,0:T(8,128)} reshape(f32[8,4,4,64,2,32]{5,4,3,2,1,0:T(2,128)} %copy.115) | data formatting | bytes 4194304 | tf_op jit(solution)/shard_map/reshape | solution.py:110
  (46 shorter events, 3.3 us)
Async XLA Ops:
  0.0 30.0 %copy-start = (s32[128,4]{0,1:T(4,128)S(1)}, s32[128,4]{0,1:T(4,128)}, u32[]{:S(2)}) copy-start(s32[128,4]{0,1:T(4,128)} %param.17) | copy-start | bytes 6148
  13.0 68.7 %all-to-all-start.1 = ((f32[8,2,128,256]{3,0,1,2:T(8,128)}), f32[8,2,128,256]{3,0,1,2:T(8,128)S(1)}, u32[]{:S(2)}, u32[]{:S(2)}) async-start(f32[8,2,128,256]{3,0,1,2:T(8,128)} %pad_maximum_fusion), calls=%async_computation.1 | async-start | bytes 4194304 | tf_op jit(solution)/shard_map/all_to_all | solution.py:164
  33.2 4.4 %copy-start.3 = (f32[64,3]{0,1:T(4,128)S(1)}, f32[64,3]{0,1:T(4,128)}, u32[]{:S(2)}) copy-start(f32[64,3]{0,1:T(4,128)} %param.22) | copy-start | bytes 2308
  33.2 4.4 %copy-start.4 = (s32[64,3]{0,1:T(4,128)S(1)}, s32[64,3]{0,1:T(4,128)}, u32[]{:S(2)}) copy-start(s32[64,3]{0,1:T(4,128)} %param.21) | copy-start | bytes 2308
  33.2 4.4 %copy-start.5 = (f32[128,3]{0,1:T(4,128)S(1)}, f32[128,3]{0,1:T(4,128)}, u32[]{:S(2)}) copy-start(f32[128,3]{0,1:T(4,128)} %param.19) | copy-start | bytes 4612
  33.2 4.4 %copy-start.6 = (s32[128,3]{0,1:T(4,128)S(1)}, s32[128,3]{0,1:T(4,128)}, u32[]{:S(2)}) copy-start(s32[128,3]{0,1:T(4,128)} %param.18) | copy-start | bytes 4612
  33.2 4.4 %copy-start.7 = (f32[128,3]{0,1:T(4,128)S(1)}, f32[128,3]{0,1:T(4,128)}, u32[]{:S(2)}) copy-start(f32[128,3]{0,1:T(4,128)} %param.23) | copy-start | bytes 4612
  37.7 53.1 %copy-start.2 = (f32[256,3]{0,1:T(4,128)S(1)}, f32[256,3]{0,1:T(4,128)}, u32[]{:S(2)}) copy-start(f32[256,3]{0,1:T(4,128)} %param.20) | copy-start | bytes 9220
  81.7 60.2 %all-to-all-start = ((f32[8,1,512,128]{3,0,1,2:T(8,128)}), f32[8,1,512,128]{3,0,1,2:T(8,128)}, u32[]{:S(2)}, u32[]{:S(2)}) async-start(f32[8,1,512,128]{3,0,1,2:T(8,128)} %copy.103), calls=%async_computation | async-start | bytes 4194304 | tf_op jit(solution)/shard_map/all_to_all | solution.py:163
  170.2 13.0 %copy-start.1 = (s32[128,4]{0,1:T(4,128)S(1)}, s32[128,4]{0,1:T(4,128)}, u32[]{:S(2)}) copy-start(s32[128,4]{0,1:T(4,128)} %param.17) | copy-start | bytes 6148
where the time goes:
time: 184 us; the launch traced here: 183 us
  waiting for transfers between devices  75.2 us (41%)
  local copies, waits for them, and re-layouts  35.9 us (20%)
  starting transfers between devices  26 us (14%)
  matrix products  24.1 us (13%)
  other arithmetic  15.4 us (8%)
  blocking collectives  3.74 us (2%)
  between operations  2.79 us (2%)
    all_to_all x1, waiting for transfers between devices, local(): lax.all_to_all(shifted, 'dev', split_axis=2, concat_axis=1, tiled=True)  44 us
    all_to_all x1, waiting for transfers between devices, local(): lax.all_to_all(level1_adj, 'dev', split_axis=2, concat_axis=1, tiled=True)  31.2 us
    all_to_all x1, starting transfers between devices, local(): lax.all_to_all(shifted, 'dev', split_axis=2, concat_axis=1, tiled=True)  17 us
    reshape x1, local copies, waits for them, and re-layouts, lower_level(): phi_done.reshape(result_shape[:-5] + (result_shape[-5] * 4, result_shape[...  13 us
    transpose x1, local copies, waits for them, and re-layouts, lower_level(): jnp.einsum('c...piju,pq->...ijqcu', theta_done, phi_map, precision=lax.Pr...  12.3 us
    dot_general x4, matrix products, upper_level(): jnp.einsum('...pbt,tu->...pbu', stacked, theta_map, precision=lax.Precisi...  9.64 us
    all_to_all x1, starting transfers between devices, local(): lax.all_to_all(level1_adj, 'dev', split_axis=2, concat_axis=1, tiled=True)  9.05 us
    dot_general x1, matrix products, lower_level(): jnp.einsum('c...piju,pq->...ijqcu', theta_done, phi_map, precision=lax.Pr...  5.21 us
  transfers between devices with their start and end apart: 2, of which 2 were waited for; matrix products, arithmetic and copies ran while one was open for 14% of the time, Pallas kernels for 0%

commit v1 on v0

v1 whole, which is shorter than its diff:
```python
import math

import jax
import jax.numpy as jnp
from jax import lax
from jax.experimental import pallas as pl
from jax.experimental.pallas import tpu as pltpu
from jax.sharding import PartitionSpec as P

PHASE_TOP = 18.85
PHASE_MID = 9.42
LATTICE = 12.57

F32 = jnp.float32
BF16 = jnp.bfloat16

EXC = 8
RN = 16
ZN = 8
PAD = 2
BASES = 4
IMAGES = 64


def iota(shape, dim):
    return lax.broadcasted_iota(jnp.int32, shape, dim)


def column(row):
    n = row.shape[1]
    square = jnp.where(iota((n, n), 0) == iota((n, n), 1), jnp.broadcast_to(row, (n, n)), 0.0)
    return jnp.sum(square, axis=1, keepdims=True)


def split(x):
    high = x.astype(BF16)
    return high, (x - high.astype(F32)).astype(BF16)


def dot3(x, w_high, w_low):
    high, low = split(x)
    out = jnp.dot(high, w_high, preferred_element_type=F32)
    out += jnp.dot(low, w_high, preferred_element_type=F32)
    out += jnp.dot(high, w_low, preferred_element_type=F32)
    return out


def bases(factor, theta, azimuth):
    sin_theta = jnp.sin(theta)
    along_x = factor * (jnp.cos(azimuth) * sin_theta)
    along_y = factor * (jnp.sin(azimuth) * sin_theta)
    cos_x, sin_x = jnp.cos(along_x), jnp.sin(along_x)
    cos_y, sin_y = jnp.cos(along_y), jnp.sin(along_y)
    return cos_x * cos_y, sin_x * sin_y, sin_x * cos_y, cos_x * sin_y


def theta_rows(index_ref, weight_ref, columns):
    samples = index_ref.shape[1]
    rows = iota((columns, samples), 0)
    total = jnp.zeros((columns, samples), F32)
    for s in range(3):
        hit = rows == jnp.broadcast_to(index_ref[s : s + 1, :], (columns, samples))
        total += jnp.where(hit, jnp.broadcast_to(weight_ref[s : s + 1, :], (columns, samples)), 0.0)
    return total


def kernel(
    top_hbm, lvl_hbm, off_ref, wgt_ref, inc_ref, child_ref, tit_ref, twt_ref, pwt_ref,
    tim_ref, twm_ref, pwm_ref,
    out_hbm,
    tin, lin, off_p, wgt_p, lattice,
    s1t, s1l, r1t, r1l, hs, hr, g1, sb, r2, ov,
    btab, wtab, btab2, wtab2, signs,
    wab_h, wab_l, wgd_h, wgd_l, w2t, w2_h, w2_l,
    xs, tq, x2, y2,
    sem_tin, sem_lin, sem_img_s, sem_img_r,
    ss_t, rs_t, ss_l, rs_l, ss_h, rs_h, ss_2, rs_2, sem_out,
):
    dev = lax.axis_index("dev")
    rhs = lax.axis_index("rhs")
    z = dev // RN
    r = dev % RN

    barrier = pltpu.get_barrier_semaphore()

    def greet_plane(o, _):
        pl.semaphore_signal(
            barrier, inc=1, device_id={"dev": z * RN + (r + o) % RN},
            device_id_type=pl.DeviceIdType.MESH,
        )
        return 0

    def greet_column(o, _):
        pl.semaphore_signal(
            barrier, inc=1, device_id={"dev": (z + o) % ZN * RN + r},
            device_id_type=pl.DeviceIdType.MESH,
        )
        return 0

    lax.fori_loop(1, RN, greet_plane, 0)
    lax.fori_loop(1, ZN, greet_column, 0)
    pl.semaphore_signal(
        barrier, inc=1, device_id={"rhs": 1 - rhs}, device_id_type=pl.DeviceIdType.MESH
    )

    def start_inputs(e, _):
        pltpu.make_async_copy(lvl_hbm.at[e], lin.at[e], sem_lin.at[e]).start()
        for p in range(2):
            for c in range(2):
                pltpu.make_async_copy(
                    top_hbm.at[e, p, :, pl.ds(c * 128, 128)], tin.at[e, p, c], sem_tin.at[e]
                ).start()
        return 0

    lax.fori_loop(0, EXC, start_inputs, 0)

    def pack_level(e):
        pltpu.make_async_copy(lin.at[e], lin.at[e], sem_lin.at[e]).wait()

        def body(q, _):
            for j in range(4):
                s1l[e, q, j] = lin[e, pl.ds(4 * q + j, ZN, stride=4 * RN), :]
            return 0

        lax.fori_loop(0, RN, body, 0)

    def pack_top(e):
        pltpu.make_async_copy(tin.at[e], tin.at[e], sem_tin.at[e]).wait()
        mine = rhs * EXC + e
        factors = []
        for p in range(2):
            for c in range(2):
                factors.append(jnp.broadcast_to(lattice[p, c, pl.ds(mine, 1), :], (ZN, 128)))

        def body(q, _):
            for p in range(2):
                s_re, s_im = factors[2 * p], factors[2 * p + 1]
                a_re = tin[e, p, 0, pl.ds(q, ZN, stride=RN), :]
                a_im = tin[e, p, 1, pl.ds(q, ZN, stride=RN), :]
                s1t[e, q, 2 * p] = s_re * a_re + s_im * a_im
                s1t[e, q, 2 * p + 1] = s_re * a_im - s_im * a_re
            return 0

        lax.fori_loop(0, RN, body, 0)

    def send_plane(e, source, target, send_sem, recv_sem, first):
        def body(o, _):
            peer = (r + o) % RN
            pltpu.make_async_remote_copy(
                src_ref=source.at[e, peer], dst_ref=target.at[e, first + r],
                send_sem=send_sem.at[e], recv_sem=recv_sem.at[e],
                device_id={"dev": z * RN + peer}, device_id_type=pl.DeviceIdType.MESH,
            ).start()
            return 0

        lax.fori_loop(1, RN, body, 0)
        pltpu.make_async_copy(source.at[e, r], target.at[e, first + r], recv_sem.at[e]).start()

    def wait_bytes(ref, sem):
        pltpu.make_async_copy(ref, ref, sem).wait()

    pack_level(0)
    pl.semaphore_wait(barrier, RN - 1 + ZN - 1 + 1)
    images = []
    for k, (source, target) in enumerate(((off_ref, off_p), (wgt_ref, wgt_p))):
        images.append(
            pltpu.make_async_remote_copy(
                src_ref=source, dst_ref=target, send_sem=sem_img_s.at[k], recv_sem=sem_img_r.at[k],
                device_id={"rhs": 1 - rhs}, device_id_type=pl.DeviceIdType.MESH,
            )
        )
        images[-1].start()
    send_plane(0, s1l, r1l, ss_l, rs_l, 0)
    pack_level(1)
    send_plane(1, s1l, r1l, ss_l, rs_l, 0)

    theta = (math.pi / 128) * (iota((8, 128), 1).astype(F32) + 0.5)
    own_phi = (2 * math.pi / 256) * (2 * dev + iota((8, 128), 0)).astype(F32)
    own_x = jnp.cos(own_phi) * jnp.sin(theta)
    own_y = jnp.sin(own_phi) * jnp.sin(theta)
    for copy in images:
        copy.wait()
    off_x, off_y, weight = [], [], []
    for offsets, weights in ((off_ref, wgt_ref), (off_p, wgt_p)):
        off_x.append(column(offsets[0:1, :].astype(F32)))
        off_y.append(column(offsets[1:2, :].astype(F32)))
        weight.append(column(weights[...]) * (float(IMAGES) ** -0.5))
    off_x = jnp.concatenate(off_x, axis=0)
    off_y = jnp.concatenate(off_y, axis=0)
    weight = jnp.concatenate(weight, axis=0)
    turn = -LATTICE * (off_x * inc_ref[0:1, :] + off_y * inc_ref[1:2, :])
    coef_re = weight * jnp.cos(turn)
    coef_im = weight * jnp.sin(turn)

    def over_images(a, b):
        return lax.dot_general(
            a, b, (((0,), (0,)), ((), ())), precision=lax.Precision.HIGHEST,
            preferred_element_type=F32,
        )

    for p in range(2):
        angle = LATTICE * (off_x * own_x[p : p + 1, :] + off_y * own_y[p : p + 1, :])
        wave_re, wave_im = jnp.cos(angle), jnp.sin(angle)
        lattice[p, 0] = over_images(coef_re, wave_re) - over_images(coef_im, wave_im)
        lattice[p, 1] = over_images(coef_re, wave_im) + over_images(coef_im, wave_re)

    def send_all(e, _):
        pack_top(e)
        send_plane(e, s1t, r1t, ss_t, rs_t, PAD)

        @pl.when(e < EXC - 2)
        def _():
            pack_level(e + 2)
            send_plane(e + 2, s1l, r1l, ss_l, rs_l, 0)

        return 0

    lax.fori_loop(0, EXC, send_all, 0)

    zeros = jnp.zeros((ZN, 128), F32)

    def clear_top(e, _):
        for k in range(PAD):
            for c in range(4):
                r1t[e, k, c] = zeros
                r1t[e, PAD + RN + k, c] = zeros
        return 0

    lax.fori_loop(0, EXC, clear_top, 0)

    def clear_mid(k, _):
        for slot in range(2):
            for i in range(4):
                g1[slot, k, i] = zeros
                g1[slot, RN + 2 * PAD + k, i] = zeros
        return 0

    lax.fori_loop(0, 2 * PAD, clear_mid, 0)

    def clear_weights(k, _):
        for s in range(3):
            for b in range(BASES):
                wtab[k, s, b] = zeros
                wtab[2 * RN + 2 * PAD + k, s, b] = zeros
                wtab2[k, s, b] = zeros
                wtab2[RN + 2 * PAD + k, s, b] = zeros
        return 0

    lax.fori_loop(0, 2 * PAD, clear_weights, 0)

    theta_b = (math.pi / 128) * (iota((32, 128), 1).astype(F32) + 0.5)
    phi_b = (2 * math.pi / 256) * (32 * z + iota((32, 128), 0)).astype(F32)
    for b, value in enumerate(bases(PHASE_TOP, theta_b, phi_b)):
        btab[b] = value
    mid_t = (iota((16, 128), 1) % 64).astype(F32)
    theta_b = (math.pi / 64) * (mid_t + 0.5)
    phi_b = (2 * math.pi / 128) * (16 * z + iota((16, 128), 0)).astype(F32)
    for b, value in enumerate(bases(PHASE_MID, theta_b, phi_b)):
        btab2[b] = value

    def weigh_top(p, _):
        for b in range(BASES):
            row = jnp.broadcast_to(btab[b, pl.ds(p, 1), :], (ZN, 128))
            for s in range(3):
                wtab[2 * PAD + p, s, b] = row * pwt_ref[s, 32 * z + p]
        return 0

    lax.fori_loop(0, 2 * RN, weigh_top, 0)

    def weigh_mid(p, _):
        for b in range(BASES):
            row = jnp.broadcast_to(btab2[b, pl.ds(p, 1), :], (ZN, 128))
            for s in range(3):
                wtab2[2 * PAD + p, s, b] = row * pwm_ref[s, 16 * z + p]
        return 0

    lax.fori_loop(0, RN, weigh_mid, 0)

    own_box = iota((ZN, 128), 1) == RN * iota((ZN, 128), 0) + r
    own_first = (4 * (RN * iota((ZN, 1), 0) + r)).astype(F32)
    places = []
    for j in range(4):
        row = jnp.broadcast_to(child_ref[j : j + 1, :].astype(F32), (ZN, 128))
        places.append(jnp.sum(jnp.where(own_box, row, 0.0), axis=1, keepdims=True) - own_first)
    for i in range(4):
        sign_x = jnp.zeros((ZN, 1), F32)
        sign_y = jnp.zeros((ZN, 1), F32)
        for j in range(4):
            here = jnp.where(places[j] == float(i), 1.0, 0.0)
            sign_x += (2.0 * (j % 2) - 1.0) * here
            sign_y += (2.0 * (j // 2) - 1.0) * here
        signs[i, 0] = jnp.broadcast_to(sign_x * sign_y, (ZN, 128))
        signs[i, 1] = jnp.broadcast_to(sign_x, (ZN, 128))
        signs[i, 2] = jnp.broadcast_to(sign_y, (ZN, 128))

    theta_t = theta_rows(tit_ref, twt_ref, 64)
    along_z = PHASE_TOP * jnp.cos((math.pi / 128) * (iota((1, 128), 1).astype(F32) + 0.5))
    with_cos = theta_t * jnp.cos(along_z)
    with_sin = theta_t * jnp.sin(along_z)

    def square(upper_left, upper_right, lower_left, lower_right):
        upper = jnp.concatenate([upper_left, upper_right], axis=1)
        lower = jnp.concatenate([lower_left, lower_right], axis=1)
        return jnp.concatenate([upper, lower], axis=0)

    wab_h[...], wab_l[...] = split(square(with_cos, with_sin, -with_sin, with_cos).T)
    wgd_h[...], wgd_l[...] = split(square(with_sin, -with_cos, with_cos, with_sin).T)

    theta_m = theta_rows(tim_ref, twm_ref, 32)
    theta_m = jnp.concatenate([theta_m, theta_m], axis=1)
    lane = iota((1, 128), 1)
    along_z = PHASE_MID * jnp.cos((math.pi / 64) * ((lane % 64).astype(F32) + 0.5))
    cos_z, sin_z = jnp.cos(along_z), jnp.sin(along_z)
    low = lane < 64
    rows = (
        (jnp.where(low, cos_z, sin_z), jnp.where(low, -sin_z, cos_z)),
        (jnp.where(low, sin_z, -cos_z), jnp.where(low, cos_z, sin_z)),
    )
    for j in range(4):
        sign_x = 2.0 * (j % 2) - 1.0
        sign_y = 2.0 * (j // 2) - 1.0
        for c in range(2):
            for b, sign in enumerate((1.0, -sign_x * sign_y, sign_x, sign_y)):
                w2t[pl.ds(64 * j + 32 * c, 32), pl.ds(128 * b, 128)] = theta_m * (
                    sign * rows[b // 2][c]
                )
    w2_h[...], w2_l[...] = split(w2t[...].T)

    def upper(e):
        wait_bytes(r1t.at[e, pl.ds(PAD, RN)], rs_t.at[e])
        wait_bytes(r1l.at[e], rs_l.at[e])

        def stencil(q, _):
            total = [[None, None] for _ in range(BASES)]
            for s in range(3):
                for h in range(2):
                    slot = q - s + PAD
                    data = [r1t[e, slot, 2 * h + c] for c in range(2)]
                    for b in range(BASES):
                        factor = wtab[2 * slot + h, s, b]
                        for c in range(2):
                            term = factor * data[c]
                            total[b][c] = term if total[b][c] is None else total[b][c] + term
            for b in range(BASES):
                for c in range(2):
                    xs[b // 2, pl.ds(144 * (b % 2) + 8 * q, 8), pl.ds(128 * c, 128)] = total[b][c]
            return 0

        lax.fori_loop(0, RN + 2, stencil, 0)
        tq[0] = dot3(xs[0], wab_h[...], wab_l[...])
        tq[1] = dot3(xs[1], wgd_h[...], wgd_l[...])

        def combine(q):
            part = [tq[b // 2, pl.ds(144 * (b % 2) + 8 * q, 8), :] for b in range(BASES)]
            return [
                part[0] - signs[i, 0] * part[1] + signs[i, 1] * part[2] + signs[i, 2] * part[3]
                for i in range(4)
            ]

        def inner(q, _):
            for i, value in enumerate(combine(q + 1)):
                g1[e % 2, 2 * PAD + q, i] = r1l[e, q, i] + value
            return 0

        lax.fori_loop(0, RN, inner, 0)
        for side, q in enumerate((0, RN + 1)):
            for i, value in enumerate(combine(q)):
                hs[e, side, i] = value
        for side, plane in enumerate(((z + ZN - 1) % ZN, (z + 1) % ZN)):
            pltpu.make_async_remote_copy(
                src_ref=hs.at[e, side], dst_ref=hr.at[e, side],
                send_sem=ss_h.at[e], recv_sem=rs_h.at[e],
                device_id={"dev": plane * RN + r}, device_id_type=pl.DeviceIdType.MESH,
            ).start()

    half = iota((ZN, 128), 1) < 64

    def lower(e):
        slot = e % 2
        wait_bytes(hr.at[e], rs_h.at[e])
        for i in range(4):
            g1[slot, 2 * PAD + RN - 1, i] += hr[e, 0, i]
            g1[slot, 2 * PAD, i] += hr[e, 1, i]

        def stencil(q, _):
            for i in range(4):
                total = [None] * BASES
                for s in range(3):
                    for h in range(2):
                        place = 2 * (q - s + PAD) + h
                        data = g1[slot, place, i]
                        for b in range(BASES):
                            term = wtab2[place, s, b] * data
                            total[b] = term if total[b] is None else total[b] + term
                for b in range(BASES):
                    x2[pl.ds(32 * q + 8 * i, 8), pl.ds(128 * b, 128)] = total[b]
            return 0

        lax.fori_loop(0, RN // 2 + 2, stencil, 0)
        y2[...] = dot3(x2[...], w2_h[...], w2_l[...])

        for m in range(5):
            first, second = (2 * m + 1, 2 * m + 2) if m < 4 else (9, 0)

            def place(i, _):
                for k in range(2):
                    a = y2[pl.ds(32 * first + 8 * i, 8), pl.ds(128 * k, 128)]
                    b = y2[pl.ds(32 * second + 8 * i, 8), pl.ds(128 * k, 128)]
                    even = jnp.where(half, a, pltpu.roll(b, 64, 1))
                    odd = jnp.where(half, pltpu.roll(a, 64, 1), b)
                    sb[e, m, pl.ds(4 * i + 2 * k, ZN, stride=16), :] = even
                    sb[e, m, pl.ds(4 * i + 2 * k + 1, ZN, stride=16), :] = odd
                return 0

            lax.fori_loop(0, 4, place, 0)

        def send(o, _):
            peer = (z + o) % ZN
            pltpu.make_async_remote_copy(
                src_ref=sb.at[e, :, pl.ds(16 * peer, 16), :], dst_ref=r2.at[e, z],
                send_sem=ss_2.at[e], recv_sem=rs_2.at[e],
                device_id={"dev": peer * RN + r}, device_id_type=pl.DeviceIdType.MESH,
            ).start()
            return 0

        lax.fori_loop(1, ZN, send, 0)
        pltpu.make_async_copy(
            sb.at[e, :, pl.ds(16 * z, 16), :], r2.at[e, z], rs_2.at[e]
        ).start()

    def levels(e, _):
        @pl.when(e < EXC)
        def _():
            upper(e)

        @pl.when(e > 0)
        def _():
            lower(e - 1)

        return 0

    lax.fori_loop(0, EXC + 1, levels, 0)

    low_half = iota((16, 128), 1) < 64

    def assemble(e, _):
        wait_bytes(r2.at[e], rs_2.at[e])
        for k in range(ZN):
            for m in range(4):
                value = r2[e, k, m]
                if m == 0:
                    value = value + jnp.where(low_half, r2[e, (k + ZN - 1) % ZN, 4], 0.0)
                if m == 3:
                    value = value + jnp.where(low_half, 0.0, r2[e, (k + 1) % ZN, 4])
                ov[e, :, pl.ds(512 * k + 128 * m, 128)] = value
        pltpu.make_async_copy(ov.at[e], out_hbm.at[e], sem_out.at[e]).start()
        return 0

    lax.fori_loop(0, EXC, assemble, 0)

    def drain(e, _):
        wait_bytes(s1l.at[e, pl.ds(0, RN - 1)], ss_l.at[e])
        wait_bytes(s1t.at[e, pl.ds(0, RN - 1)], ss_t.at[e])
        wait_bytes(hs.at[e], ss_h.at[e])
        wait_bytes(r2.at[e, pl.ds(0, ZN - 1)], ss_2.at[e])
        pltpu.make_async_copy(ov.at[e], out_hbm.at[e], sem_out.at[e]).wait()
        return 0

    lax.fori_loop(0, EXC, drain, 0)


def local(
    top_adj,
    level1_adj,
    image_offsets,
    image_weights,
    incidence,
    child_list,
    theta_index_top,
    theta_weight_top,
    phi_weight_top,
    theta_index_mid,
    theta_weight_mid,
    phi_weight_mid,
):
    vmem = pl.BlockSpec(memory_space=pltpu.VMEM)
    smem = pl.BlockSpec(memory_space=pltpu.SMEM)
    anywhere = pl.BlockSpec(memory_space=pl.ANY)
    dma = pltpu.SemaphoreType.DMA
    return pl.pallas_call(
        kernel,
        out_shape=jax.ShapeDtypeStruct((EXC, 16, 4096), F32),
        in_specs=[
            anywhere, anywhere, vmem, vmem, vmem, vmem, vmem, vmem, smem, vmem, vmem, smem,
        ],
        out_specs=anywhere,
        scratch_shapes=[
            pltpu.VMEM((EXC, 2, 2, 128, 128), F32),
            pltpu.VMEM((EXC, 512, 128), F32),
            pltpu.VMEM((2, 32), jnp.int32),
            pltpu.VMEM((1, 32), F32),
            pltpu.VMEM((2, 2, 16, 128), F32),
            pltpu.VMEM((EXC, RN, 4, ZN, 128), F32),
            pltpu.VMEM((EXC, RN, 4, ZN, 128), F32),
            pltpu.VMEM((EXC, RN + 2 * PAD, 4, ZN, 128), F32),
            pltpu.VMEM((EXC, RN, 4, ZN, 128), F32),
            pltpu.VMEM((EXC, 2, 4, ZN, 128), F32),
            pltpu.VMEM((EXC, 2, 4, ZN, 128), F32),
            pltpu.VMEM((2, RN + 4 * PAD, 4, ZN, 128), F32),
            pltpu.VMEM((EXC, 5, 128, 128), F32),
            pltpu.VMEM((EXC, ZN, 5, 16, 128), F32),
            pltpu.VMEM((EXC, 16, 4096), F32),
            pltpu.VMEM((BASES, 32, 128), F32),
            pltpu.VMEM((2 * RN + 4 * PAD, 3, BASES, ZN, 128), F32),
            pltpu.VMEM((BASES, 16, 128), F32),
            pltpu.VMEM((RN + 4 * PAD, 3, BASES, ZN, 128), F32),
            pltpu.VMEM((4, 3, ZN, 128), F32),
            pltpu.VMEM((256, 128), BF16),
            pltpu.VMEM((256, 128), BF16),
            pltpu.VMEM((256, 128), BF16),
            pltpu.VMEM((256, 128), BF16),
            pltpu.VMEM((256, 512), F32),
            pltpu.VMEM((512, 256), BF16),
            pltpu.VMEM((512, 256), BF16),
            pltpu.VMEM((2, 288, 256), F32),
            pltpu.VMEM((2, 288, 128), F32),
            pltpu.VMEM((320, 512), F32),
            pltpu.VMEM((320, 256), F32),
            dma((EXC,)), dma((EXC,)), dma((2,)), dma((2,)),
            dma((EXC,)), dma((EXC,)), dma((EXC,)), dma((EXC,)),
            dma((EXC,)), dma((EXC,)), dma((EXC,)), dma((EXC,)), dma((EXC,)),
        ],
        compiler_params=pltpu.CompilerParams(
            collective_id=0, has_side_effects=True, vmem_limit_bytes=50 * 2**20
        ),
        name="two_stage_adjoint",
    )(
        top_adj,
        level1_adj.reshape(EXC, 512, 128),
        image_offsets.T,
        image_weights.reshape(1, 32),
        incidence.T,
        child_list.T,
        theta_index_top.T,
        theta_weight_top.T,
        phi_weight_top.T,
        theta_index_mid.T,
        theta_weight_mid.T,
        phi_weight_mid.T,
    )


def solution(mesh):
    placed = (
        P("rhs", "dev", None, None),
        P("rhs", "dev", None, None),
        P("rhs", None),
        P("rhs"),
        P(),
        P(),
        P(),
        P(),
        P(),
        P(),
        P(),
        P(),
    )
    return jax.shard_map(
        local, mesh=mesh, in_specs=placed, out_specs=P("rhs", "dev", None), check_vma=False
    )
```

time: 184 us -> 102 us (0.55)
  Pallas kernels: 0 us -> 93.6 us
  waiting for transfers between devices: 75.2 us -> 0 us
  local copies, waits for them, and re-layouts: 35.9 us -> 8.11 us
  starting transfers between devices: 26 us -> 0 us
  matrix products: 24.1 us -> 0 us
  other arithmetic: 15.4 us -> 0 us
  blocking collectives: 3.74 us -> 0 us
  between operations: 2.79 us -> 0.02 us
    pallas_call x0 -> x1, Pallas kernels: none -> 93.6 us  [local(): pl.pallas_call(kernel, out_shape=jax.ShapeDtypeStruct((EXC, 16, 4096), F3...]
    all_to_all x2 -> x0, waiting for transfers between devices: 75.2 us -> none  [the longest x1 44 us: local(): lax.all_to_all(shifted, 'dev', split_axis=2, concat_axis=1, tiled=True)]
    all_to_all x2 -> x0, starting transfers between devices: 26 us -> none  [the longest x1 17 us: local(): lax.all_to_all(shifted, 'dev', split_axis=2, concat_axis=1, tiled=True)]
    dot_general x10 -> x0, matrix products: 24.1 us -> none  [the longest x4 9.64 us: upper_level(): jnp.einsum('...pbt,tu->...pbu', stacked, theta_map, precision=lax.Precisi...]
    reshape x1 -> x0, local copies, waits for them, and re-layouts: 13 us -> none  [lower_level(): phi_done.reshape(result_shape[:-5] + (result_shape[-5] * 4, result_shape[...]
    transpose x1 -> x0, local copies, waits for them, and re-layouts: 12.3 us -> none  [lower_level(): jnp.einsum('c...piju,pq->...ijqcu', theta_done, phi_map, precision=lax.Pr...]
    unnamed x18 -> x21, local copies, waits for them, and re-layouts: 4.28 us -> 8.11 us
    all_gather x1 -> x0, blocking collectives: 3.74 us -> none  [side_by_side(): out = lax.all_gather(both, axis, axis=dim, tiled=True)]
  transfers between devices with their start and end apart: 2 -> 0, of which waited for: 2 -> 0; matrix products, arithmetic and copies ran while one was open for 14% -> 0% of each run, Pallas kernels for 0% -> 0%
where the time goes in v1:
time: 102 us
  Pallas kernels  93.6 us (92%)
  local copies, waits for them, and re-layouts  8.11 us (8%)
    pallas_call x1, Pallas kernels, local(): pl.pallas_call(kernel, out_shape=jax.ShapeDtypeStruct((EXC, 16, 4096), F3...  93.6 us
    unnamed x21, local copies, waits for them, and re-layouts  8.11 us

profile of v1, /device:TPU:1, one launch (start us, length us, event | category | flops | bytes accessed | tf_op | source)
XLA Modules:
  0.0 101.7 jit_solution(11971780791210841831)
XLA Ops:
  0.0 0.0 copy-start
  0.0 0.7 copy-done
  0.7 0.0 copy-start.1
  0.7 0.7 copy-done.1
  1.4 0.0 copy-start.2
  1.4 0.7 copy-done.2
  2.1 0.0 copy-start.3
  2.1 0.7 copy-done.3
  2.7 0.0 copy-start.4
  2.7 0.7 copy-done.4
  3.4 0.0 copy-start.5
  3.4 0.7 copy-done.5
  4.1 0.0 copy-start.6
  4.1 0.7 copy-done.6
  4.8 0.0 copy-start.7
  4.8 0.7 copy-done.7
  5.5 0.0 copy-start.8
  5.5 0.7 copy-done.8
  6.1 0.0 copy-start.9
  6.1 0.7 copy-done.9
  6.8 93.6 %two_stage_adjoint.1 = f32[8,16,4096]{2,1,0:T(8,128)S(1)} custom-call(f32[8,2,128,256]{3,2,1,0:T(8,128)} %top_hbm.1, f32[8,512,128]{2,1,0:T(8,128)} %bitcast.21, s32[2,32]{1,0:T(2,128)S(1)} %bitcast.18, f32[1,32]{1,0:T(1,128)S(1)} %bitcast.20, f32[2,16]{1,0:T(2,128)S(1)} %bitcast.19, s32[4,128]{1,0:T(4,128)S(1)} %bitcast.12, s32[3,128]{1,0:T(4,128)S(1)} %bitcast.13, ...), custom_call_target="tpu_custom_call" | custom-call | tf_op jit(solution)/shard_map/two_stage_adjoint/pallas_call | solution.py:490
  100.4 1.3 %copy.14 = f32[8,16,4096]{2,1,0:T(8,128)} copy(f32[8,16,4096]{2,1,0:T(8,128)S(1)} %two_stage_adjoint.1) | data formatting | bytes 4194304
Async XLA Ops:
  0.0 0.7 copy-start
  0.7 0.7 copy-start.1
  1.4 0.7 copy-start.2
  2.1 0.7 copy-start.3
  2.7 0.7 copy-start.4
  3.4 0.7 copy-start.5
  4.1 0.7 copy-start.6
  4.8 0.7 copy-start.7
  5.5 0.7 copy-start.8
  6.1 0.7 copy-start.9

commit v2 on v1

--- a/solution.py
+++ b/solution.py
@@ -19,7 +19,9 @@
 ZN = 8
 PAD = 2
 BASES = 4
+EXT = RN + 4
 IMAGES = 64
+AHEAD = 3
 
 
 def iota(shape, dim):
@@ -45,12 +47,29 @@
     return out
 
 
+def sincos(x):
+    turns = jnp.floor(x * (2.0 / math.pi) + 0.5)
+    rest = ((x - turns * 1.5703125) - turns * 4.837512969970703e-4) - turns * 7.549789954891882e-8
+    z = rest * rest
+    sine = ((-1.9515295891e-4 * z + 8.3321608736e-3) * z - 1.6666654611e-1) * z * rest + rest
+    cosine = (
+        ((2.443315711809948e-5 * z - 1.388731625493765e-3) * z + 4.166664568298827e-2) * z * z
+        - 0.5 * z + 1.0
+    )
+    quadrant = turns.astype(jnp.int32) & 3
+    odd = (quadrant & 1) == 1
+    out_sin = jnp.where(odd, cosine, sine)
+    out_cos = jnp.where(odd, sine, cosine)
+    out_sin = jnp.where(quadrant >= 2, -out_sin, out_sin)
+    out_cos = jnp.where(((quadrant + 1) & 2) == 2, -out_cos, out_cos)
+    return out_sin, out_cos
+
+
 def bases(factor, theta, azimuth):
-    sin_theta = jnp.sin(theta)
-    along_x = factor * (jnp.cos(azimuth) * sin_theta)
-    along_y = factor * (jnp.sin(azimuth) * sin_theta)
-    cos_x, sin_x = jnp.cos(along_x), jnp.sin(along_x)
-    cos_y, sin_y = jnp.cos(along_y), jnp.sin(along_y)
+    sin_theta, _ = sincos(theta)
+    sin_phi, cos_phi = sincos(azimuth)
+    sin_x, cos_x = sincos(factor * (cos_phi * sin_theta))
+    sin_y, cos_y = sincos(factor * (sin_phi * sin_theta))
     return cos_x * cos_y, sin_x * sin_y, sin_x * cos_y, cos_x * sin_y
 
 
@@ -65,15 +84,16 @@
 
 
 def kernel(
-    top_hbm, lvl_hbm, off_ref, wgt_ref, inc_ref, child_ref, tit_ref, twt_ref, pwt_ref,
-    tim_ref, twm_ref, pwm_ref,
+    top_hbm, lvl_hbm, off_hbm, wgt_hbm, inc_hbm, child_hbm, tit_hbm, twt_hbm, pwt_hbm,
+    tim_hbm, twm_hbm, pwm_hbm,
     out_hbm,
+    off_ref, wgt_ref, inc_ref, child_ref, tit_ref, twt_ref, pwt_ref, tim_ref, twm_ref, pwm_ref,
     tin, lin, off_p, wgt_p, lattice,
-    s1t, s1l, r1t, r1l, hs, hr, g1, sb, r2, ov,
+    s1t, s1l, r1t, r1l, hr, ge, sb, r2, ov,
     btab, wtab, btab2, wtab2, signs,
     wab_h, wab_l, wgd_h, wgd_l, w2t, w2_h, w2_l,
     xs, tq, x2, y2,
-    sem_tin, sem_lin, sem_img_s, sem_img_r,
+    sem_small, sem_tin, sem_lin, sem_img_s, sem_img_r,
     ss_t, rs_t, ss_l, rs_l, ss_h, rs_h, ss_2, rs_2, sem_out,
 ):
     dev = lax.axis_index("dev")
@@ -102,6 +122,17 @@
     pl.semaphore_signal(
         barrier, inc=1, device_id={"rhs": 1 - rhs}, device_id_type=pl.DeviceIdType.MESH
     )
+
+    smalls = [
+        pltpu.make_async_copy(source, target, sem_small.at[k])
+        for k, (source, target) in enumerate((
+            (off_hbm, off_ref), (wgt_hbm, wgt_ref), (inc_hbm, inc_ref), (child_hbm, child_ref),
+            (tit_hbm, tit_ref), (twt_hbm, twt_ref), (pwt_hbm, pwt_ref), (tim_hbm, tim_ref),
+            (twm_hbm, twm_ref), (pwm_hbm, pwm_ref),
+        ))
+    ]
+    for copy in smalls[:3]:
+        copy.start()
 
     def start_inputs(e, _):
         pltpu.make_async_copy(lvl_hbm.at[e], lin.at[e], sem_lin.at[e]).start()
@@ -113,6 +144,8 @@
         return 0
 
     lax.fori_loop(0, EXC, start_inputs, 0)
+    for copy in smalls[3:]:
+        copy.start()
 
     def pack_level(e):
         pltpu.make_async_copy(lin.at[e], lin.at[e], sem_lin.at[e]).wait()
@@ -160,6 +193,8 @@
         pltpu.make_async_copy(ref, ref, sem).wait()
 
     pack_level(0)
+    for copy in smalls[:3]:
+        copy.wait()
     pl.semaphore_wait(barrier, RN - 1 + ZN - 1 + 1)
     images = []
     for k, (source, target) in enumerate(((off_ref, off_p), (wgt_ref, wgt_p))):
@@ -171,13 +206,13 @@
         )
         images[-1].start()
     send_plane(0, s1l, r1l, ss_l, rs_l, 0)
-    pack_level(1)
-    send_plane(1, s1l, r1l, ss_l, rs_l, 0)
 
     theta = (math.pi / 128) * (iota((8, 128), 1).astype(F32) + 0.5)
     own_phi = (2 * math.pi / 256) * (2 * dev + iota((8, 128), 0)).astype(F32)
-    own_x = jnp.cos(own_phi) * jnp.sin(theta)
-    own_y = jnp.sin(own_phi) * jnp.sin(theta)
+    sin_theta, _ = sincos(theta)
+    sin_phi, cos_phi = sincos(own_phi)
+    own_x = cos_phi * sin_theta
+    own_y = sin_phi * sin_theta
     for copy in images:
         copy.wait()
     off_x, off_y, weight = [], [], []
@@ -189,8 +224,7 @@
     off_y = jnp.concatenate(off_y, axis=0)
     weight = jnp.concatenate(weight, axis=0)
     turn = -LATTICE * (off_x * inc_ref[0:1, :] + off_y * inc_ref[1:2, :])
-    coef_re = weight * jnp.cos(turn)
-    coef_im = weight * jnp.sin(turn)
+    coef_im, coef_re = (weight * value for value in sincos(turn))
 
     def over_images(a, b):
         return lax.dot_general(
@@ -200,22 +234,21 @@
 
     for p in range(2):
         angle = LATTICE * (off_x * own_x[p : p + 1, :] + off_y * own_y[p : p + 1, :])
-        wave_re, wave_im = jnp.cos(angle), jnp.sin(angle)
+        wave_im, wave_re = sincos(angle)
         lattice[p, 0] = over_images(coef_re, wave_re) - over_images(coef_im, wave_im)
         lattice[p, 1] = over_images(coef_re, wave_im) + over_images(coef_im, wave_re)
 
-    def send_all(e, _):
+    pack_top(0)
+    send_plane(0, s1t, r1t, ss_t, rs_t, PAD)
+
+    def send_both(e, _):
+        pack_level(e)
+        send_plane(e, s1l, r1l, ss_l, rs_l, 0)
         pack_top(e)
         send_plane(e, s1t, r1t, ss_t, rs_t, PAD)
-
-        @pl.when(e < EXC - 2)
-        def _():
-            pack_level(e + 2)
-            send_plane(e + 2, s1l, r1l, ss_l, rs_l, 0)
-
-        return 0
-
-    lax.fori_loop(0, EXC, send_all, 0)
+        return 0
+
+    lax.fori_loop(1, AHEAD, send_both, 0)
 
     zeros = jnp.zeros((ZN, 128), F32)
 
@@ -228,33 +261,24 @@
 
     lax.fori_loop(0, EXC, clear_top, 0)
 
-    def clear_mid(k, _):
-        for slot in range(2):
-            for i in range(4):
-                g1[slot, k, i] = zeros
-                g1[slot, RN + 2 * PAD + k, i] = zeros
-        return 0
-
-    lax.fori_loop(0, 2 * PAD, clear_mid, 0)
-
     def clear_weights(k, _):
         for s in range(3):
             for b in range(BASES):
                 wtab[k, s, b] = zeros
                 wtab[2 * RN + 2 * PAD + k, s, b] = zeros
-                wtab2[k, s, b] = zeros
-                wtab2[RN + 2 * PAD + k, s, b] = zeros
         return 0
 
     lax.fori_loop(0, 2 * PAD, clear_weights, 0)
 
+    for copy in smalls[3:]:
+        copy.wait()
     theta_b = (math.pi / 128) * (iota((32, 128), 1).astype(F32) + 0.5)
     phi_b = (2 * math.pi / 256) * (32 * z + iota((32, 128), 0)).astype(F32)
     for b, value in enumerate(bases(PHASE_TOP, theta_b, phi_b)):
         btab[b] = value
-    mid_t = (iota((16, 128), 1) % 64).astype(F32)
+    mid_t = (iota((24, 128), 1) % 64).astype(F32)
     theta_b = (math.pi / 64) * (mid_t + 0.5)
-    phi_b = (2 * math.pi / 128) * (16 * z + iota((16, 128), 0)).astype(F32)
+    phi_b = (2 * math.pi / 128) * (16 * z - 2 + iota((24, 128), 0)).astype(F32)
     for b, value in enumerate(bases(PHASE_MID, theta_b, phi_b)):
         btab2[b] = value
 
@@ -271,10 +295,10 @@
         for b in range(BASES):
             row = jnp.broadcast_to(btab2[b, pl.ds(p, 1), :], (ZN, 128))
             for s in range(3):
-                wtab2[2 * PAD + p, s, b] = row * pwm_ref[s, 16 * z + p]
-        return 0
-
-    lax.fori_loop(0, RN, weigh_mid, 0)
+                wtab2[p, s, b] = row * pwm_ref[s, (16 * z - 2 + p + 128) % 128]
+        return 0
+
+    lax.fori_loop(0, EXT, weigh_mid, 0)
 
     own_box = iota((ZN, 128), 1) == RN * iota((ZN, 128), 0) + r
     own_first = (4 * (RN * iota((ZN, 1), 0) + r)).astype(F32)
@@ -294,9 +318,10 @@
         signs[i, 2] = jnp.broadcast_to(sign_y, (ZN, 128))
 
     theta_t = theta_rows(tit_ref, twt_ref, 64)
-    along_z = PHASE_TOP * jnp.cos((math.pi / 128) * (iota((1, 128), 1).astype(F32) + 0.5))
-    with_cos = theta_t * jnp.cos(along_z)
-    with_sin = theta_t * jnp.sin(along_z)
+    along_z = PHASE_TOP * sincos((math.pi / 128) * (iota((1, 128), 1).astype(F32) + 0.5))[1]
+    sin_z, cos_z = sincos(along_z)
+    with_cos = theta_t * cos_z
+    with_sin = theta_t * sin_z
 
     def square(upper_left, upper_right, lower_left, lower_right):
         upper = jnp.concatenate([upper_left, upper_right], axis=1)
@@ -309,8 +334,8 @@
     theta_m = theta_rows(tim_ref, twm_ref, 32)
     theta_m = jnp.concatenate([theta_m, theta_m], axis=1)
     lane = iota((1, 128), 1)
-    along_z = PHASE_MID * jnp.cos((math.pi / 64) * ((lane % 64).astype(F32) + 0.5))
-    cos_z, sin_z = jnp.cos(along_z), jnp.sin(along_z)
+    along_z = PHASE_MID * sincos((math.pi / 64) * ((lane % 64).astype(F32) + 0.5))[1]
+    sin_z, cos_z = sincos(along_z)
     low = lane < 64
     rows = (
         (jnp.where(low, cos_z, sin_z), jnp.where(low, -sin_z, cos_z)),
@@ -359,16 +384,16 @@
 
         def inner(q, _):
             for i, value in enumerate(combine(q + 1)):
-                g1[e % 2, 2 * PAD + q, i] = r1l[e, q, i] + value
+                ge[e, 2 + q, i] = r1l[e, q, i] + value
             return 0
 
         lax.fori_loop(0, RN, inner, 0)
-        for side, q in enumerate((0, RN + 1)):
+        for q in (0, RN + 1):
             for i, value in enumerate(combine(q)):
-                hs[e, side, i] = value
+                ge[e, 1 + q, i] = value
         for side, plane in enumerate(((z + ZN - 1) % ZN, (z + 1) % ZN)):
             pltpu.make_async_remote_copy(
-                src_ref=hs.at[e, side], dst_ref=hr.at[e, side],
+                src_ref=ge.at[e, pl.ds(1 + 15 * side, 3)], dst_ref=hr.at[e, side],
                 send_sem=ss_h.at[e], recv_sem=rs_h.at[e],
                 device_id={"dev": plane * RN + r}, device_id_type=pl.DeviceIdType.MESH,
             ).start()
@@ -376,19 +401,23 @@
     half = iota((ZN, 128), 1) < 64
 
     def lower(e):
-        slot = e % 2
+        wait_bytes(ge.at[e, pl.ds(0, 6)], ss_h.at[e])
         wait_bytes(hr.at[e], rs_h.at[e])
         for i in range(4):
-            g1[slot, 2 * PAD + RN - 1, i] += hr[e, 0, i]
-            g1[slot, 2 * PAD, i] += hr[e, 1, i]
+            ge[e, 0, i] = hr[e, 1, 0, i]
+            ge[e, 1, i] += hr[e, 1, 1, i]
+            ge[e, 2, i] += hr[e, 1, 2, i]
+            ge[e, RN + 1, i] += hr[e, 0, 0, i]
+            ge[e, RN + 2, i] += hr[e, 0, 1, i]
+            ge[e, RN + 3, i] = hr[e, 0, 2, i]
 
         def stencil(q, _):
             for i in range(4):
                 total = [None] * BASES
                 for s in range(3):
                     for h in range(2):
-                        place = 2 * (q - s + PAD) + h
-                        data = g1[slot, place, i]
+                        place = 2 * (q - s + 2) + h
+                        data = ge[e, place, i]
                         for b in range(BASES):
                             term = wtab2[place, s, b] * data
                             total[b] = term if total[b] is None else total[b] + term
@@ -396,20 +425,20 @@
                     x2[pl.ds(32 * q + 8 * i, 8), pl.ds(128 * b, 128)] = total[b]
             return 0
 
-        lax.fori_loop(0, RN // 2 + 2, stencil, 0)
+        lax.fori_loop(0, RN // 2, stencil, 0)
         y2[...] = dot3(x2[...], w2_h[...], w2_l[...])
 
-        for m in range(5):
-            first, second = (2 * m + 1, 2 * m + 2) if m < 4 else (9, 0)
+        for m in range(4):
 
             def place(i, _):
                 for k in range(2):
-                    a = y2[pl.ds(32 * first + 8 * i, 8), pl.ds(128 * k, 128)]
-                    b = y2[pl.ds(32 * second + 8 * i, 8), pl.ds(128 * k, 128)]
+                    a = y2[pl.ds(64 * m + 8 * i, 8), pl.ds(128 * k, 128)]
+                    b = y2[pl.ds(64 * m + 32 + 8 * i, 8), pl.ds(128 * k, 128)]
                     even = jnp.where(half, a, pltpu.roll(b, 64, 1))
                     odd = jnp.where(half, pltpu.roll(a, 64, 1), b)
-                    sb[e, m, pl.ds(4 * i + 2 * k, ZN, stride=16), :] = even
-                    sb[e, m, pl.ds(4 * i + 2 * k + 1, ZN, stride=16), :] = odd
+                    row = 32 * (i // 2) + 8 * m + 4 * (i % 2) + 2 * k
+                    sb[e, pl.ds(row, ZN, stride=64), :] = even
+                    sb[e, pl.ds(row + 1, ZN, stride=64), :] = odd
                 return 0
 
             lax.fori_loop(0, 4, place, 0)
@@ -417,7 +446,7 @@
         def send(o, _):
             peer = (z + o) % ZN
             pltpu.make_async_remote_copy(
-                src_ref=sb.at[e, :, pl.ds(16 * peer, 16), :], dst_ref=r2.at[e, z],
+                src_ref=sb.at[e, pl.ds(64 * peer, 64), :], dst_ref=r2.at[e, z],
                 send_sem=ss_2.at[e], recv_sem=rs_2.at[e],
                 device_id={"dev": peer * RN + r}, device_id_type=pl.DeviceIdType.MESH,
             ).start()
@@ -425,10 +454,14 @@
 
         lax.fori_loop(1, ZN, send, 0)
         pltpu.make_async_copy(
-            sb.at[e, :, pl.ds(16 * z, 16), :], r2.at[e, z], rs_2.at[e]
+            sb.at[e, pl.ds(64 * z, 64), :], r2.at[e, z], rs_2.at[e]
         ).start()
 
     def levels(e, _):
+        @pl.when(e < EXC - AHEAD)
+        def _():
+            send_both(e + AHEAD, 0)
+
         @pl.when(e < EXC)
         def _():
             upper(e)
@@ -441,18 +474,14 @@
 
     lax.fori_loop(0, EXC + 1, levels, 0)
 
-    low_half = iota((16, 128), 1) < 64
-
     def assemble(e, _):
         wait_bytes(r2.at[e], rs_2.at[e])
         for k in range(ZN):
-            for m in range(4):
-                value = r2[e, k, m]
-                if m == 0:
-                    value = value + jnp.where(low_half, r2[e, (k + ZN - 1) % ZN, 4], 0.0)
-                if m == 3:
-                    value = value + jnp.where(low_half, 0.0, r2[e, (k + 1) % ZN, 4])
-                ov[e, :, pl.ds(512 * k + 128 * m, 128)] = value
+            for i in range(2):
+                for m in range(4):
+                    ov[e, pl.ds(8 * i, 8), pl.ds(512 * k + 128 * m, 128)] = r2[
+                        e, k, pl.ds(32 * i + 8 * m, 8), :
+                    ]
         pltpu.make_async_copy(ov.at[e], out_hbm.at[e], sem_out.at[e]).start()
         return 0
 
@@ -461,8 +490,7 @@
     def drain(e, _):
         wait_bytes(s1l.at[e, pl.ds(0, RN - 1)], ss_l.at[e])
         wait_bytes(s1t.at[e, pl.ds(0, RN - 1)], ss_t.at[e])
-        wait_bytes(hs.at[e], ss_h.at[e])
-        wait_bytes(r2.at[e, pl.ds(0, ZN - 1)], ss_2.at[e])
+        wait_bytes(sb.at[e, pl.ds(0, 64 * (ZN - 1))], ss_2.at[e])
         pltpu.make_async_copy(ov.at[e], out_hbm.at[e], sem_out.at[e]).wait()
         return 0
 
@@ -483,18 +511,25 @@
     theta_weight_mid,
     phi_weight_mid,
 ):
-    vmem = pl.BlockSpec(memory_space=pltpu.VMEM)
-    smem = pl.BlockSpec(memory_space=pltpu.SMEM)
     anywhere = pl.BlockSpec(memory_space=pl.ANY)
+    hbm = pl.BlockSpec(memory_space=pltpu.HBM)
     dma = pltpu.SemaphoreType.DMA
     return pl.pallas_call(
         kernel,
         out_shape=jax.ShapeDtypeStruct((EXC, 16, 4096), F32),
-        in_specs=[
-            anywhere, anywhere, vmem, vmem, vmem, vmem, vmem, vmem, smem, vmem, vmem, smem,
-        ],
+        in_specs=[hbm] * 12,
         out_specs=anywhere,
         scratch_shapes=[
+            pltpu.VMEM((2, 32), jnp.int32),
+            pltpu.VMEM((1, 32), F32),
+            pltpu.VMEM((2, 16), F32),
+            pltpu.VMEM((4, 128), jnp.int32),
+            pltpu.VMEM((3, 128), jnp.int32),
+            pltpu.VMEM((3, 128), F32),
+            pltpu.SMEM((3, 256), F32),
+            pltpu.VMEM((3, 64), jnp.int32),
+            pltpu.VMEM((3, 64), F32),
+            pltpu.SMEM((3, 128), F32),
             pltpu.VMEM((EXC, 2, 2, 128, 128), F32),
             pltpu.VMEM((EXC, 512, 128), F32),
             pltpu.VMEM((2, 32), jnp.int32),
@@ -504,16 +539,15 @@
             pltpu.VMEM((EXC, RN, 4, ZN, 128), F32),
             pltpu.VMEM((EXC, RN + 2 * PAD, 4, ZN, 128), F32),
             pltpu.VMEM((EXC, RN, 4, ZN, 128), F32),
-            pltpu.VMEM((EXC, 2, 4, ZN, 128), F32),
-            pltpu.VMEM((EXC, 2, 4, ZN, 128), F32),
-            pltpu.VMEM((2, RN + 4 * PAD, 4, ZN, 128), F32),
-            pltpu.VMEM((EXC, 5, 128, 128), F32),
-            pltpu.VMEM((EXC, ZN, 5, 16, 128), F32),
+            pltpu.VMEM((EXC, 2, 3, 4, ZN, 128), F32),
+            pltpu.VMEM((EXC, EXT, 4, ZN, 128), F32),
+            pltpu.VMEM((EXC, 512, 128), F32),
+            pltpu.VMEM((EXC, ZN, 64, 128), F32),
             pltpu.VMEM((EXC, 16, 4096), F32),
             pltpu.VMEM((BASES, 32, 128), F32),
             pltpu.VMEM((2 * RN + 4 * PAD, 3, BASES, ZN, 128), F32),
-            pltpu.VMEM((BASES, 16, 128), F32),
-            pltpu.VMEM((RN + 4 * PAD, 3, BASES, ZN, 128), F32),
+            pltpu.VMEM((BASES, 24, 128), F32),
+            pltpu.VMEM((EXT, 3, BASES, ZN, 128), F32),
             pltpu.VMEM((4, 3, ZN, 128), F32),
             pltpu.VMEM((256, 128), BF16),
             pltpu.VMEM((256, 128), BF16),
@@ -524,9 +558,9 @@
             pltpu.VMEM((512, 256), BF16),
             pltpu.VMEM((2, 288, 256), F32),
             pltpu.VMEM((2, 288, 128), F32),
-            pltpu.VMEM((320, 512), F32),
-            pltpu.VMEM((320, 256), F32),
-            dma((EXC,)), dma((EXC,)), dma((2,)), dma((2,)),
+            pltpu.VMEM((256, 512), F32),
+            pltpu.VMEM((256, 256), F32),
+            dma((10,)), dma((EXC,)), dma((EXC,)), dma((2,)), dma((2,)),
             dma((EXC,)), dma((EXC,)), dma((EXC,)), dma((EXC,)),
             dma((EXC,)), dma((EXC,)), dma((EXC,)), dma((EXC,)), dma((EXC,)),
         ],
@@ -534,20 +568,23 @@
             collective_id=0, has_side_effects=True, vmem_limit_bytes=50 * 2**20
         ),
         name="two_stage_adjoint",
-    )(
-        top_adj,
-        level1_adj.reshape(EXC, 512, 128),
-        image_offsets.T,
-        image_weights.reshape(1, 32),
-        incidence.T,
-        child_list.T,
-        theta_index_top.T,
-        theta_weight_top.T,
-        phi_weight_top.T,
-        theta_index_mid.T,
-        theta_weight_mid.T,
-        phi_weight_mid.T,
-    )
+    )(*(
+        pltpu.with_memory_space_constraint(x, pltpu.HBM)
+        for x in (
+            top_adj,
+            level1_adj.reshape(EXC, 512, 128),
+            image_offsets.T,
+            image_weights.reshape(1, 32),
+            incidence.T,
+            child_list.T,
+            theta_index_top.T,
+            theta_weight_top.T,
+            phi_weight_top.T,
+            theta_index_mid.T,
+            theta_weight_mid.T,
+            phi_weight_mid.T,
+        )
+    ))
 
 
 def solution(mesh):

time: 102 us -> 84.8 us (0.83)
  Pallas kernels: 93.6 us -> 83.4 us
  local copies, waits for them, and re-layouts: 8.11 us -> 1.32 us
    pallas_call x1, Pallas kernels: 93.6 us -> 83.4 us  [local(): pl.pallas_call(kernel, out_shape=jax.ShapeDtypeStruct((EXC, 16, 4096), F3...]
    unnamed x21 -> x1, local copies, waits for them, and re-layouts: 8.11 us -> 1.32 us
where the time goes in v2:
time: 84.8 us; the launch traced here: 84.7 us
  Pallas kernels  83.4 us (98%)
  local copies, waits for them, and re-layouts  1.32 us (2%)
    pallas_call x1, Pallas kernels, local(): pl.pallas_call(kernel, out_shape=jax.ShapeDtypeStruct((EXC, 16, 4096), F3...  83.4 us

profile of v2, /device:TPU:1, one launch (start us, length us, event | category | flops | bytes accessed | tf_op | source)
XLA Modules:
  0.0 84.7 jit_solution(8159637067748558100)
XLA Ops:
  0.0 83.4 %two_stage_adjoint.1 = f32[8,16,4096]{2,1,0:T(8,128)S(1)} custom-call(f32[8,2,128,256]{3,2,1,0:T(8,128)} %top_hbm.1, f32[8,512,128]{2,1,0:T(8,128)} %bitcast.11, s32[2,32]{1,0:T(2,128)} %bitcast.19, f32[1,32]{1,0:T(1,128)} %bitcast.21, f32[2,16]{1,0:T(2,128)} %bitcast.20, s32[4,128]{1,0:T(4,128)} %bitcast.13, s32[3,128]{1,0:T(4,128)} %bitcast.14, ...), custom_call_target="tpu_custom_call" | custom-call | tf_op jit(solution)/shard_map/two_stage_adjoint/pallas_call | solution.py:517
  83.4 1.3 %copy.14 = f32[8,16,4096]{2,1,0:T(8,128)} copy(f32[8,16,4096]{2,1,0:T(8,128)S(1)} %two_stage_adjoint.1) | data formatting | bytes 4194304

commit v3 on v2

--- a/solution.py
+++ b/solution.py
@@ -19,9 +19,16 @@
 ZN = 8
 PAD = 2
 BASES = 4
-EXT = RN + 4
 IMAGES = 64
-AHEAD = 3
+AHEAD = 1
+LAG = 2
+ROWS = 72
+
+
+FAR_FIRST = (
+    (2, 2), (2, 3), (1, 2), (3, 3), (3, 2), (1, 3), (2, 0), (0, 2), (2, 1), (0, 3),
+    (1, 0), (3, 1), (3, 0), (1, 1), (0, 1),
+)
 
 
 def iota(shape, dim):
@@ -88,13 +95,13 @@
     tim_hbm, twm_hbm, pwm_hbm,
     out_hbm,
     off_ref, wgt_ref, inc_ref, child_ref, tit_ref, twt_ref, pwt_ref, tim_ref, twm_ref, pwm_ref,
-    tin, lin, off_p, wgt_p, lattice,
-    s1t, s1l, r1t, r1l, hr, ge, sb, r2, ov,
-    btab, wtab, btab2, wtab2, signs,
+    tin, lin, lat_own, lat_far, lattice,
+    s1t, s1l, r1t, r1l, sb, r2, gq, ot, ov,
+    btab, wtab, wb, wtab2, signs,
     wab_h, wab_l, wgd_h, wgd_l, w2t, w2_h, w2_l,
     xs, tq, x2, y2,
     sem_small, sem_tin, sem_lin, sem_img_s, sem_img_r,
-    ss_t, rs_t, ss_l, rs_l, ss_h, rs_h, ss_2, rs_2, sem_out,
+    ss_t, rs_t, ss_l, rs_l, ss_2, rs_2, sem_out,
 ):
     dev = lax.axis_index("dev")
     rhs = lax.axis_index("rhs")
@@ -159,11 +166,10 @@
 
     def pack_top(e):
         pltpu.make_async_copy(tin.at[e], tin.at[e], sem_tin.at[e]).wait()
-        mine = rhs * EXC + e
         factors = []
         for p in range(2):
             for c in range(2):
-                factors.append(jnp.broadcast_to(lattice[p, c, pl.ds(mine, 1), :], (ZN, 128)))
+                factors.append(jnp.broadcast_to(lattice[p, c, pl.ds(e, 1), :], (ZN, 128)))
 
         def body(q, _):
             for p in range(2):
@@ -177,67 +183,65 @@
         lax.fori_loop(0, RN, body, 0)
 
     def send_plane(e, source, target, send_sem, recv_sem, first):
-        def body(o, _):
-            peer = (r + o) % RN
+        for over, across in FAR_FIRST:
+            peer = (
+                (r // 4 + over) % 4 * 4 + (r // 2 + across // 2) % 2 * 2 + (r + across) % 2
+            )
             pltpu.make_async_remote_copy(
                 src_ref=source.at[e, peer], dst_ref=target.at[e, first + r],
                 send_sem=send_sem.at[e], recv_sem=recv_sem.at[e],
                 device_id={"dev": z * RN + peer}, device_id_type=pl.DeviceIdType.MESH,
             ).start()
-            return 0
-
-        lax.fori_loop(1, RN, body, 0)
         pltpu.make_async_copy(source.at[e, r], target.at[e, first + r], recv_sem.at[e]).start()
 
     def wait_bytes(ref, sem):
         pltpu.make_async_copy(ref, ref, sem).wait()
 
-    pack_level(0)
     for copy in smalls[:3]:
         copy.wait()
-    pl.semaphore_wait(barrier, RN - 1 + ZN - 1 + 1)
-    images = []
-    for k, (source, target) in enumerate(((off_ref, off_p), (wgt_ref, wgt_p))):
-        images.append(
-            pltpu.make_async_remote_copy(
-                src_ref=source, dst_ref=target, send_sem=sem_img_s.at[k], recv_sem=sem_img_r.at[k],
-                device_id={"rhs": 1 - rhs}, device_id_type=pl.DeviceIdType.MESH,
-            )
-        )
-        images[-1].start()
-    send_plane(0, s1l, r1l, ss_l, rs_l, 0)
-
     theta = (math.pi / 128) * (iota((8, 128), 1).astype(F32) + 0.5)
     own_phi = (2 * math.pi / 256) * (2 * dev + iota((8, 128), 0)).astype(F32)
     sin_theta, _ = sincos(theta)
     sin_phi, cos_phi = sincos(own_phi)
     own_x = cos_phi * sin_theta
     own_y = sin_phi * sin_theta
-    for copy in images:
-        copy.wait()
-    off_x, off_y, weight = [], [], []
-    for offsets, weights in ((off_ref, wgt_ref), (off_p, wgt_p)):
-        off_x.append(column(offsets[0:1, :].astype(F32)))
-        off_y.append(column(offsets[1:2, :].astype(F32)))
-        weight.append(column(weights[...]) * (float(IMAGES) ** -0.5))
-    off_x = jnp.concatenate(off_x, axis=0)
-    off_y = jnp.concatenate(off_y, axis=0)
-    weight = jnp.concatenate(weight, axis=0)
+    off_x = column(off_ref[0:1, :].astype(F32))
+    off_y = column(off_ref[1:2, :].astype(F32))
+    weight = column(wgt_ref[...]) * (float(IMAGES) ** -0.5)
     turn = -LATTICE * (off_x * inc_ref[0:1, :] + off_y * inc_ref[1:2, :])
     coef_im, coef_re = (weight * value for value in sincos(turn))
-
-    def over_images(a, b):
-        return lax.dot_general(
-            a, b, (((0,), (0,)), ((), ())), precision=lax.Precision.HIGHEST,
+    waves = []
+    for p in range(2):
+        angle = LATTICE * (off_x * own_x[p : p + 1, :] + off_y * own_y[p : p + 1, :])
+        waves.extend(reversed(sincos(angle)))
+    waves = jnp.concatenate(waves, axis=1)
+    with_re, with_im = (
+        lax.dot_general(
+            coef, waves, (((0,), (0,)), ((), ())), precision=lax.Precision.HIGHEST,
             preferred_element_type=F32,
         )
-
+        for coef in (coef_re, coef_im)
+    )
     for p in range(2):
-        angle = LATTICE * (off_x * own_x[p : p + 1, :] + off_y * own_y[p : p + 1, :])
-        wave_im, wave_re = sincos(angle)
-        lattice[p, 0] = over_images(coef_re, wave_re) - over_images(coef_im, wave_im)
-        lattice[p, 1] = over_images(coef_re, wave_im) + over_images(coef_im, wave_re)
-
+        at = 256 * p
+        total = (
+            with_re[:, at : at + 128] - with_im[:, at + 128 : at + 256],
+            with_re[:, at + 128 : at + 256] + with_im[:, at : at + 128],
+        )
+        for c in range(2):
+            for k in range(2):
+                lat_own[k, p, c] = total[c][EXC * k : EXC * (k + 1), :]
+
+    pack_level(0)
+    pl.semaphore_wait(barrier, RN - 1 + ZN - 1 + 1)
+    swap = pltpu.make_async_remote_copy(
+        src_ref=lat_own.at[1 - rhs], dst_ref=lat_far, send_sem=sem_img_s, recv_sem=sem_img_r,
+        device_id={"rhs": 1 - rhs}, device_id_type=pl.DeviceIdType.MESH,
+    )
+    swap.start()
+    send_plane(0, s1l, r1l, ss_l, rs_l, 0)
+    swap.wait()
+    lattice[...] = lat_own[rhs] + lat_far[...]
     pack_top(0)
     send_plane(0, s1t, r1t, ss_t, rs_t, PAD)
 
@@ -276,11 +280,16 @@
     phi_b = (2 * math.pi / 256) * (32 * z + iota((32, 128), 0)).astype(F32)
     for b, value in enumerate(bases(PHASE_TOP, theta_b, phi_b)):
         btab[b] = value
-    mid_t = (iota((24, 128), 1) % 64).astype(F32)
+    mid_t = (iota((144, 128), 1) % 64).astype(F32)
     theta_b = (math.pi / 64) * (mid_t + 0.5)
-    phi_b = (2 * math.pi / 128) * (16 * z - 2 + iota((24, 128), 0)).astype(F32)
-    for b, value in enumerate(bases(PHASE_MID, theta_b, phi_b)):
-        btab2[b] = value
+    mid_p = (iota((144, 128), 0) + 120) % 128
+    mid_bases = bases(PHASE_MID, theta_b, (2 * math.pi / 128) * mid_p.astype(F32))
+    own_lane = mid_p == iota((144, 128), 1)
+    for s in range(3):
+        row = jnp.broadcast_to(pwm_ref[s : s + 1, :], (144, 128))
+        weights = jnp.sum(jnp.where(own_lane, row, 0.0), axis=1, keepdims=True)
+        for b in range(BASES):
+            wb[s, b] = weights * mid_bases[b]
 
     def weigh_top(p, _):
         for b in range(BASES):
@@ -291,14 +300,16 @@
 
     lax.fori_loop(0, 2 * RN, weigh_top, 0)
 
-    def weigh_mid(p, _):
-        for b in range(BASES):
-            row = jnp.broadcast_to(btab2[b, pl.ds(p, 1), :], (ZN, 128))
+    def weigh_mid(g, _):
+        for odd in range(2):
             for s in range(3):
-                wtab2[p, s, b] = row * pwm_ref[s, (16 * z - 2 + p + 128) % 128]
-        return 0
-
-    lax.fori_loop(0, EXT, weigh_mid, 0)
+                for h in range(2):
+                    first = 32 * g + 2 * (odd - s) + 10 + h
+                    for b in range(BASES):
+                        wtab2[g, odd, s, h, b] = wb[s, b, pl.ds(first, 8, stride=4), :]
+        return 0
+
+    lax.fori_loop(0, 4, weigh_mid, 0)
 
     own_box = iota((ZN, 128), 1) == RN * iota((ZN, 128), 0) + r
     own_first = (4 * (RN * iota((ZN, 1), 0) + r)).astype(F32)
@@ -384,78 +395,83 @@
 
         def inner(q, _):
             for i, value in enumerate(combine(q + 1)):
-                ge[e, 2 + q, i] = r1l[e, q, i] + value
+                sb[e, pl.ds(16 * i + q, ZN, stride=ROWS), :] = r1l[e, q, i] + value
             return 0
 
         lax.fori_loop(0, RN, inner, 0)
-        for q in (0, RN + 1):
+        for side, q in enumerate((0, RN + 1)):
             for i, value in enumerate(combine(q)):
-                ge[e, 1 + q, i] = value
-        for side, plane in enumerate(((z + ZN - 1) % ZN, (z + 1) % ZN)):
-            pltpu.make_async_remote_copy(
-                src_ref=ge.at[e, pl.ds(1 + 15 * side, 3)], dst_ref=hr.at[e, side],
-                send_sem=ss_h.at[e], recv_sem=rs_h.at[e],
-                device_id={"dev": plane * RN + r}, device_id_type=pl.DeviceIdType.MESH,
-            ).start()
-
-    half = iota((ZN, 128), 1) < 64
-
-    def lower(e):
-        wait_bytes(ge.at[e, pl.ds(0, 6)], ss_h.at[e])
-        wait_bytes(hr.at[e], rs_h.at[e])
-        for i in range(4):
-            ge[e, 0, i] = hr[e, 1, 0, i]
-            ge[e, 1, i] += hr[e, 1, 1, i]
-            ge[e, 2, i] += hr[e, 1, 2, i]
-            ge[e, RN + 1, i] += hr[e, 0, 0, i]
-            ge[e, RN + 2, i] += hr[e, 0, 1, i]
-            ge[e, RN + 3, i] = hr[e, 0, 2, i]
-
-        def stencil(q, _):
-            for i in range(4):
-                total = [None] * BASES
-                for s in range(3):
-                    for h in range(2):
-                        place = 2 * (q - s + 2) + h
-                        data = ge[e, place, i]
-                        for b in range(BASES):
-                            term = wtab2[place, s, b] * data
-                            total[b] = term if total[b] is None else total[b] + term
-                for b in range(BASES):
-                    x2[pl.ds(32 * q + 8 * i, 8), pl.ds(128 * b, 128)] = total[b]
-            return 0
-
-        lax.fori_loop(0, RN // 2, stencil, 0)
-        y2[...] = dot3(x2[...], w2_h[...], w2_l[...])
-
-        for m in range(4):
-
-            def place(i, _):
-                for k in range(2):
-                    a = y2[pl.ds(64 * m + 8 * i, 8), pl.ds(128 * k, 128)]
-                    b = y2[pl.ds(64 * m + 32 + 8 * i, 8), pl.ds(128 * k, 128)]
-                    even = jnp.where(half, a, pltpu.roll(b, 64, 1))
-                    odd = jnp.where(half, pltpu.roll(a, 64, 1), b)
-                    row = 32 * (i // 2) + 8 * m + 4 * (i % 2) + 2 * k
-                    sb[e, pl.ds(row, ZN, stride=64), :] = even
-                    sb[e, pl.ds(row + 1, ZN, stride=64), :] = odd
-                return 0
-
-            lax.fori_loop(0, 4, place, 0)
-
-        def send(o, _):
+                sb[e, pl.ds(64 + 2 * i + side, ZN, stride=ROWS), :] = value
+
+        for o in (4, 3, 5, 2, 6, 1, 7):
             peer = (z + o) % ZN
             pltpu.make_async_remote_copy(
-                src_ref=sb.at[e, pl.ds(64 * peer, 64), :], dst_ref=r2.at[e, z],
+                src_ref=sb.at[e, pl.ds(ROWS * peer, ROWS), :],
+                dst_ref=r2.at[e, pl.ds(ROWS * z, ROWS), :],
                 send_sem=ss_2.at[e], recv_sem=rs_2.at[e],
                 device_id={"dev": peer * RN + r}, device_id_type=pl.DeviceIdType.MESH,
             ).start()
+        pltpu.make_async_copy(
+            sb.at[e, pl.ds(ROWS * z, ROWS), :], r2.at[e, pl.ds(ROWS * z, ROWS), :], rs_2.at[e]
+        ).start()
+
+    half = iota((8, 128), 1) < 64
+
+    def lower(e):
+        wait_bytes(r2.at[e], rs_2.at[e])
+
+        def gather(k, _):
+            for i in range(4):
+                gq[i, pl.ds(8 + 16 * k, 16), :] = r2[e, pl.ds(ROWS * k + 16 * i, 16), :]
             return 0
 
-        lax.fori_loop(1, ZN, send, 0)
-        pltpu.make_async_copy(
-            sb.at[e, pl.ds(64 * z, 64), :], r2.at[e, z], rs_2.at[e]
-        ).start()
+        lax.fori_loop(0, ZN, gather, 0)
+        for i in range(4):
+            gq[i, pl.ds(0, 8), :] = zeros
+            gq[i, pl.ds(136, 8), :] = zeros
+            for side in range(2):
+                halo = r2[e, pl.ds(64 + 2 * i + side, ZN, stride=ROWS), :]
+                gq[i, pl.ds(7 + 17 * side, ZN, stride=16), :] += halo
+            gq[i, pl.ds(135, 1), :] += gq[i, pl.ds(7, 1), :]
+            gq[i, pl.ds(8, 1), :] += gq[i, pl.ds(136, 1), :]
+            gq[i, pl.ds(6, 2), :] = gq[i, pl.ds(134, 2), :]
+            gq[i, pl.ds(136, 2), :] = gq[i, pl.ds(8, 2), :]
+
+        def stencil(g, _):
+            for i in range(4):
+                data = {
+                    (shift, h): gq[i, pl.ds(32 * g + 2 * shift + 10 + h, 8, stride=4), :]
+                    for shift in range(-2, 2)
+                    for h in range(2)
+                }
+                for odd in range(2):
+                    for b in range(BASES):
+                        total = None
+                        for s in range(3):
+                            for h in range(2):
+                                term = wtab2[g, odd, s, h, b] * data[odd - s, h]
+                                total = term if total is None else total + term
+                        x2[pl.ds(128 * odd + 32 * i + 8 * g, 8), pl.ds(128 * b, 128)] = total
+            return 0
+
+        lax.fori_loop(0, 4, stencil, 0)
+        y2[...] = dot3(x2[...], w2_h[...], w2_l[...])
+
+        def place(g, _):
+            for i in range(4):
+                for k in range(2):
+                    a = y2[pl.ds(32 * i + 8 * g, 8), pl.ds(128 * k, 128)]
+                    b = y2[pl.ds(128 + 32 * i + 8 * g, 8), pl.ds(128 * k, 128)]
+                    row = 256 * (i // 2) + 64 * g + 4 * (i % 2) + 2 * k
+                    ot[pl.ds(row, 8, stride=8), :] = jnp.where(half, a, pltpu.roll(b, 64, 1))
+                    ot[pl.ds(row + 1, 8, stride=8), :] = jnp.where(half, pltpu.roll(a, 64, 1), b)
+            return 0
+
+        lax.fori_loop(0, 4, place, 0)
+        for k in range(2):
+            for m in range(32):
+                ov[e, pl.ds(8 * k, 8), pl.ds(128 * m, 128)] = ot[pl.ds(256 * k + 8 * m, 8), :]
+        pltpu.make_async_copy(ov.at[e], out_hbm.at[e], sem_out.at[e]).start()
 
     def levels(e, _):
         @pl.when(e < EXC - AHEAD)
@@ -466,31 +482,18 @@
         def _():
             upper(e)
 
-        @pl.when(e > 0)
+        @pl.when(e >= LAG)
         def _():
-            lower(e - 1)
-
-        return 0
-
-    lax.fori_loop(0, EXC + 1, levels, 0)
-
-    def assemble(e, _):
-        wait_bytes(r2.at[e], rs_2.at[e])
-        for k in range(ZN):
-            for i in range(2):
-                for m in range(4):
-                    ov[e, pl.ds(8 * i, 8), pl.ds(512 * k + 128 * m, 128)] = r2[
-                        e, k, pl.ds(32 * i + 8 * m, 8), :
-                    ]
-        pltpu.make_async_copy(ov.at[e], out_hbm.at[e], sem_out.at[e]).start()
-        return 0
-
-    lax.fori_loop(0, EXC, assemble, 0)
+            lower(e - LAG)
+
+        return 0
+
+    lax.fori_loop(0, EXC + LAG, levels, 0)
 
     def drain(e, _):
         wait_bytes(s1l.at[e, pl.ds(0, RN - 1)], ss_l.at[e])
         wait_bytes(s1t.at[e, pl.ds(0, RN - 1)], ss_t.at[e])
-        wait_bytes(sb.at[e, pl.ds(0, 64 * (ZN - 1))], ss_2.at[e])
+        wait_bytes(sb.at[e, pl.ds(0, ROWS * (ZN - 1))], ss_2.at[e])
         pltpu.make_async_copy(ov.at[e], out_hbm.at[e], sem_out.at[e]).wait()
         return 0
 
@@ -529,25 +532,25 @@
             pltpu.SMEM((3, 256), F32),
             pltpu.VMEM((3, 64), jnp.int32),
             pltpu.VMEM((3, 64), F32),
-            pltpu.SMEM((3, 128), F32),
+            pltpu.VMEM((3, 128), F32),
             pltpu.VMEM((EXC, 2, 2, 128, 128), F32),
             pltpu.VMEM((EXC, 512, 128), F32),
-            pltpu.VMEM((2, 32), jnp.int32),
-            pltpu.VMEM((1, 32), F32),
-            pltpu.VMEM((2, 2, 16, 128), F32),
+            pltpu.VMEM((2, 2, 2, EXC, 128), F32),
+            pltpu.VMEM((2, 2, EXC, 128), F32),
+            pltpu.VMEM((2, 2, EXC, 128), F32),
             pltpu.VMEM((EXC, RN, 4, ZN, 128), F32),
             pltpu.VMEM((EXC, RN, 4, ZN, 128), F32),
             pltpu.VMEM((EXC, RN + 2 * PAD, 4, ZN, 128), F32),
             pltpu.VMEM((EXC, RN, 4, ZN, 128), F32),
-            pltpu.VMEM((EXC, 2, 3, 4, ZN, 128), F32),
-            pltpu.VMEM((EXC, EXT, 4, ZN, 128), F32),
-            pltpu.VMEM((EXC, 512, 128), F32),
-            pltpu.VMEM((EXC, ZN, 64, 128), F32),
+            pltpu.VMEM((EXC, ZN * ROWS, 128), F32),
+            pltpu.VMEM((EXC, ZN * ROWS, 128), F32),
+            pltpu.VMEM((4, 144, 128), F32),
+            pltpu.VMEM((512, 128), F32),
             pltpu.VMEM((EXC, 16, 4096), F32),
             pltpu.VMEM((BASES, 32, 128), F32),
             pltpu.VMEM((2 * RN + 4 * PAD, 3, BASES, ZN, 128), F32),
-            pltpu.VMEM((BASES, 24, 128), F32),
-            pltpu.VMEM((EXT, 3, BASES, ZN, 128), F32),
+            pltpu.VMEM((3, BASES, 144, 128), F32),
+            pltpu.VMEM((4, 2, 3, 2, BASES, 8, 128), F32),
             pltpu.VMEM((4, 3, ZN, 128), F32),
             pltpu.VMEM((256, 128), BF16),
             pltpu.VMEM((256, 128), BF16),
@@ -560,9 +563,9 @@
             pltpu.VMEM((2, 288, 128), F32),
             pltpu.VMEM((256, 512), F32),
             pltpu.VMEM((256, 256), F32),
-            dma((10,)), dma((EXC,)), dma((EXC,)), dma((2,)), dma((2,)),
+            dma((10,)), dma((EXC,)), dma((EXC,)), dma(()), dma(()),
             dma((EXC,)), dma((EXC,)), dma((EXC,)), dma((EXC,)),
-            dma((EXC,)), dma((EXC,)), dma((EXC,)), dma((EXC,)), dma((EXC,)),
+            dma((EXC,)), dma((EXC,)), dma((EXC,)),
         ],
         compiler_params=pltpu.CompilerParams(
             collective_id=0, has_side_effects=True, vmem_limit_bytes=50 * 2**20

time: 84.8 us -> 77.3 us (0.912)
  Pallas kernels: 83.4 us -> 75.9 us
    pallas_call x1, Pallas kernels: 83.4 us -> 75.9 us  [local(): pl.pallas_call(kernel, out_shape=jax.ShapeDtypeStruct((EXC, 16, 4096), F3...]
where the time goes in v3:
time: 77.3 us
  Pallas kernels  75.9 us (98%)
  local copies, waits for them, and re-layouts  1.32 us (2%)
    pallas_call x1, Pallas kernels, local(): pl.pallas_call(kernel, out_shape=jax.ShapeDtypeStruct((EXC, 16, 4096), F3...  75.9 us

profile of v3, /device:TPU:1, one launch (start us, length us, event | category | flops | bytes accessed | tf_op | source)
XLA Modules:
  0.0 77.3 jit_solution(12116569182552614960)
XLA Ops:
  0.0 75.9 %two_stage_adjoint.1 = f32[8,16,4096]{2,1,0:T(8,128)S(1)} custom-call(f32[8,2,128,256]{3,2,1,0:T(8,128)} %top_hbm.1, f32[8,512,128]{2,1,0:T(8,128)} %bitcast.11, s32[2,32]{1,0:T(2,128)} %bitcast.19, f32[1,32]{1,0:T(1,128)} %bitcast.21, f32[2,16]{1,0:T(2,128)} %bitcast.20, s32[4,128]{1,0:T(4,128)} %bitcast.13, s32[3,128]{1,0:T(4,128)} %bitcast.14, ...), custom_call_target="tpu_custom_call" | custom-call | tf_op jit(solution)/shard_map/two_stage_adjoint/pallas_call | solution.py:520
  75.9 1.3 %copy.14 = f32[8,16,4096]{2,1,0:T(8,128)} copy(f32[8,16,4096]{2,1,0:T(8,128)S(1)} %two_stage_adjoint.1) | data formatting | bytes 4194304

commit v4 on v3

--- a/solution.py
+++ b/solution.py
@@ -246,10 +246,10 @@
     send_plane(0, s1t, r1t, ss_t, rs_t, PAD)
 
     def send_both(e, _):
+        pack_top(e)
+        send_plane(e, s1t, r1t, ss_t, rs_t, PAD)
         pack_level(e)
         send_plane(e, s1l, r1l, ss_l, rs_l, 0)
-        pack_top(e)
-        send_plane(e, s1t, r1t, ss_t, rs_t, PAD)
         return 0
 
     lax.fori_loop(1, AHEAD, send_both, 0)
@@ -364,7 +364,6 @@
 
     def upper(e):
         wait_bytes(r1t.at[e, pl.ds(PAD, RN)], rs_t.at[e])
-        wait_bytes(r1l.at[e], rs_l.at[e])
 
         def stencil(q, _):
             total = [[None, None] for _ in range(BASES)]
@@ -382,7 +381,7 @@
                     xs[b // 2, pl.ds(144 * (b % 2) + 8 * q, 8), pl.ds(128 * c, 128)] = total[b][c]
             return 0
 
-        lax.fori_loop(0, RN + 2, stencil, 0)
+        lax.fori_loop(0, RN + 2, stencil, 0, unroll=2)
         tq[0] = dot3(xs[0], wab_h[...], wab_l[...])
         tq[1] = dot3(xs[1], wgd_h[...], wgd_l[...])
 
@@ -398,7 +397,8 @@
                 sb[e, pl.ds(16 * i + q, ZN, stride=ROWS), :] = r1l[e, q, i] + value
             return 0
 
-        lax.fori_loop(0, RN, inner, 0)
+        wait_bytes(r1l.at[e], rs_l.at[e])
+        lax.fori_loop(0, RN, inner, 0, unroll=2)
         for side, q in enumerate((0, RN + 1)):
             for i, value in enumerate(combine(q)):
                 sb[e, pl.ds(64 + 2 * i + side, ZN, stride=ROWS), :] = value
@@ -454,7 +454,7 @@
                         x2[pl.ds(128 * odd + 32 * i + 8 * g, 8), pl.ds(128 * b, 128)] = total
             return 0
 
-        lax.fori_loop(0, 4, stencil, 0)
+        lax.fori_loop(0, 4, stencil, 0, unroll=2)
         y2[...] = dot3(x2[...], w2_h[...], w2_l[...])
 
         def place(g, _):
@@ -467,7 +467,7 @@
                     ot[pl.ds(row + 1, 8, stride=8), :] = jnp.where(half, pltpu.roll(a, 64, 1), b)
             return 0
 
-        lax.fori_loop(0, 4, place, 0)
+        lax.fori_loop(0, 4, place, 0, unroll=2)
         for k in range(2):
             for m in range(32):
                 ov[e, pl.ds(8 * k, 8), pl.ds(128 * m, 128)] = ot[pl.ds(256 * k + 8 * m, 8), :]

time: 77.3 us -> 77 us (level)
  no operation moved by 1% of the time
where the time goes in v4:
time: 77 us; the launch traced here: 76.9 us
  Pallas kernels  75.6 us (98%)
  local copies, waits for them, and re-layouts  1.32 us (2%)
    pallas_call x1, Pallas kernels, local(): pl.pallas_call(kernel, out_shape=jax.ShapeDtypeStruct((EXC, 16, 4096), F3...  75.6 us

profile of v4, /device:TPU:1, one launch (start us, length us, event | category | flops | bytes accessed | tf_op | source)
XLA Modules:
  0.0 76.9 jit_solution(18274711906389765445)
XLA Ops:
  0.0 75.6 %two_stage_adjoint.1 = f32[8,16,4096]{2,1,0:T(8,128)S(1)} custom-call(f32[8,2,128,256]{3,2,1,0:T(8,128)} %top_hbm.1, f32[8,512,128]{2,1,0:T(8,128)} %bitcast.11, s32[2,32]{1,0:T(2,128)} %bitcast.19, f32[1,32]{1,0:T(1,128)} %bitcast.21, f32[2,16]{1,0:T(2,128)} %bitcast.20, s32[4,128]{1,0:T(4,128)} %bitcast.13, s32[3,128]{1,0:T(4,128)} %bitcast.14, ...), custom_call_target="tpu_custom_call" | custom-call | tf_op jit(solution)/shard_map/two_stage_adjoint/pallas_call | solution.py:520
  75.6 1.3 %copy.14 = f32[8,16,4096]{2,1,0:T(8,128)} copy(f32[8,16,4096]{2,1,0:T(8,128)S(1)} %two_stage_adjoint.1) | data formatting | bytes 4194304
